TPU v7x, 256 devices: a whole 4x4x8 slice. The times are simulated.
256 devices in a mesh: loop: 16 (over y_hi, x, core), stack: 16 (over y_lo, z).
Axes of the slice: x: 4, y: 4 (y_hi: 2, y_lo: 2; y = y_hi * 2 + y_lo), z: 8, core: 2. Of those that a mesh axis runs over, the one named last changes fastest.
Arguments:
- spectra: bfloat16 [512, 2, 32, 2048], P('stack', None, None, 'loop'), may hold values from -6 to 6
- channel_loc: int32 [2048], P('loop'), may hold values from 0 to 4095, as said below
- channel_valid: int32 [2048], P('loop'), may hold values 0 or 1
- bin_owner: int32 [128], replicated, may hold values from 0 to 15, as said below
Outputs:
- linear_stack: float32 [16, 16, 1024], P('stack', 'loop')
- phase_stack: float32 [16, 16, 1024], P('stack', 'loop')
Inputs may be any that keep to these rules, and one draw needn't show every extreme that they name: `channel_loc`: strictly increasing along the channels; channel c lies at 2 c or 2 c + 1, the first at 0 and the last at 4095. `bin_owner`: at most 16 bins share an owner; some owner holds exactly 16.
All inputs are finite; a program needn't handle non-finite values. No bound on the sum of `channel_valid` on one device may be relied on, other than what follows from the above.
Results may differ from a plain program's by a relative error of at most 0.003.
Values may be sent and summed in bfloat16 or wider, within the bound.
No kernel may reach another device: no remote copies, remote signals or barrier semaphores. Data moves between devices by JAX's collectives and lax.ppermute only.
A program may use at most 64 MiB of HBM per device.

v0:
```python
import math

import jax
import jax.numpy as jnp
from jax import lax
from jax.sharding import PartitionSpec as P

BCAP = 16


def lag_matrix(freq_count):
    freq_ids = jnp.arange(freq_count, dtype=jnp.int32)
    lag_ids = jnp.arange(2 * freq_count, dtype=jnp.int32) - freq_count
    turn_count = freq_ids[:, None] * lag_ids[None, :] % (2 * freq_count)
    phase_angle = turn_count.astype(jnp.float32) * (math.pi / freq_count)
    bin_weight = jnp.where(freq_ids == 0, 1.0, 2.0).astype(jnp.float32)[:, None]
    return jnp.concatenate(
        [bin_weight * jnp.cos(phase_angle), -bin_weight * jnp.sin(phase_angle)], 0
    )


def normalize(series):
    return series / jnp.sqrt(jnp.mean(series * series, axis=-1, keepdims=True) + 1e-06)


def finish(linear_re, linear_im, phase_re, phase_im):
    coherence = phase_re * phase_re + phase_im * phase_im
    matrix = lag_matrix(linear_re.shape[1])
    linear = jnp.dot(
        jnp.concatenate([linear_re, linear_im], 1), matrix, precision=lax.Precision.HIGHEST
    )
    weighted = jnp.dot(
        jnp.concatenate([linear_re * coherence, linear_im * coherence], 1),
        matrix,
        precision=lax.Precision.HIGHEST,
    )
    return (normalize(linear), normalize(weighted))


def accumulate(
    running, left_side, visiting, group_id, factor, own_loc, own_valid, chan_table, bin_width
):
    channels = visiting.shape[3]
    freq_dev = visiting.shape[0]
    bin_count = running.shape[1]
    visit_loc = lax.dynamic_slice_in_dim(chan_table[0], group_id * channels, channels)
    visit_valid = lax.dynamic_slice_in_dim(chan_table[1], group_id * channels, channels).astype(
        jnp.float32
    )
    row_count = 32
    window = min(bin_count, (2 * row_count + 2 * channels) // bin_width + 2)
    window_ids = jnp.arange(window, dtype=jnp.int32)
    for first_row in range(0, channels, row_count):
        products = jnp.einsum(
            "fkpsa,fpsb->fkab",
            left_side[..., first_row : first_row + row_count],
            visiting,
            preferred_element_type=jnp.float32,
        )
        loc_gap = visit_loc[None, :] - own_loc[first_row : first_row + row_count, None]
        orient = jnp.where(loc_gap > 0, 1.0, -1.0)
        weight = (
            jnp.where(
                loc_gap != 0,
                own_valid[first_row : first_row + row_count, None] * visit_valid[None, :],
                0.0,
            )
            * factor
        )
        pair_bin = jnp.abs(loc_gap) // bin_width
        window_start = jnp.clip(jnp.min(pair_bin), 0, bin_count - window)
        labels = window_start + window_ids
        onehot = (
            jnp.where(labels[:, None, None] == pair_bin[None, :, :], weight[None, :, :], 0.0)
            .astype(jnp.bfloat16)
            .reshape(window, row_count * channels)
        )
        real_part = products[:, 0]
        imag_part = products[:, 1]
        magnitude = jnp.maximum(jnp.sqrt(real_part * real_part + imag_part * imag_part), 1.0)
        imag_part = imag_part * orient
        components = jnp.stack(
            [real_part, imag_part, real_part / magnitude, imag_part / magnitude], 1
        ).astype(jnp.bfloat16)
        components = components.reshape(freq_dev * 4, row_count * channels)
        binned = lax.dot_general(
            components, onehot, (((1,), (1,)), ((), ())), preferred_element_type=jnp.float32
        )
        current = lax.dynamic_slice_in_dim(running, window_start, window, 1)
        running = lax.dynamic_update_slice_in_dim(running, current + binned, window_start, 1)
    return running


def on_device(spectra, channel_loc, channel_valid, bin_owner):
    stack_size = lax.axis_size("stack")
    channels = spectra.shape[3]
    freq_dev = spectra.shape[0]
    bin_count = bin_owner.shape[0]
    chan_table = lax.all_gather(jnp.stack([channel_loc, channel_valid]), "loop", axis=1, tiled=True)
    bin_width = 2 * chan_table.shape[1] // bin_count
    left_side = jnp.stack([spectra, jnp.stack([spectra[:, 1], -spectra[:, 0]], 1)], 1)
    own_valid = channel_valid.astype(jnp.float32)
    empty_sum = jnp.zeros((freq_dev * 4, bin_count), jnp.float32)

    def add_group(running, visiting, group_id, factor):
        return accumulate(
            running,
            left_side,
            visiting,
            group_id,
            factor,
            channel_loc,
            own_valid,
            chan_table,
            bin_width,
        )

    block_in = lax.all_gather(spectra, "loop", axis=3, tiled=True)
    shard_count = block_in.shape[3] // channels

    def one_shard(shard_index, current):
        visiting = lax.dynamic_slice_in_dim(block_in, shard_index * channels, channels, 3)
        return add_group(current, visiting, shard_index, 0.5)

    running = lax.fori_loop(0, shard_count, one_shard, empty_sum)
    labels = jnp.arange(bin_count, dtype=jnp.int32)
    same_owner = bin_owner[:, None] == bin_owner[None, :]
    earlier = labels[None, :] < labels[:, None]
    slot_rank = jnp.sum((same_owner & earlier).astype(jnp.int32), axis=1)
    slot_column = slot_rank * stack_size + bin_owner
    placement = (
        slot_column[:, None] == jnp.arange(BCAP * stack_size, dtype=jnp.int32)[None, :]
    ).astype(jnp.float32)
    packed = jnp.einsum("bc,rb->cr", placement, running, precision=lax.Precision.HIGHEST).reshape(
        BCAP, stack_size, freq_dev * 4
    )
    shares = lax.psum_scatter(packed, "loop", scatter_dimension=0, tiled=True)
    owned_rows = lax.all_to_all(shares, "stack", split_axis=1, concat_axis=2, tiled=True)
    row_total = owned_rows.shape[0]
    bin_sums = owned_rows.reshape(row_total, -1, 4)
    linear, weighted = finish(
        bin_sums[:, :, 0], bin_sums[:, :, 1], bin_sums[:, :, 2], bin_sums[:, :, 3]
    )
    return (linear.reshape(1, row_total, -1), weighted.reshape(1, row_total, -1))


def solution(mesh):
    in_specs = (P("stack", None, None, "loop"), P("loop"), P("loop"), P())
    out_specs = (P("stack", "loop", None), P("stack", "loop", None))
    return jax.shard_map(
        on_device, mesh=mesh, in_specs=in_specs, out_specs=out_specs, check_vma=False
    )
```

profile of v0, /device:TPU:1, one launch (start us, length us, event | category | flops | bytes accessed | tf_op | source)
XLA Modules:
  0.0 476.4 jit_solution(2361688066530951271)
XLA Ops:
  9.3 3.2 copy.19
  12.4 25.7 %all_gather.6 = s32[2,2048]{1,0:T(2,128)S(1)} all-gather(s32[2,128]{1,0:T(2,128)S(1)} %pad_add_fusion), channel_id=1, replica_groups=mesh['loop'=16,'stack'=16] {'loop'}, dimensions={1}, use_global_device_ids=true | all-gather | bytes 17408 | tf_op jit(solution)/shard_map/all_gather | solution.py:99
  38.3 60.7 %all-gather.2.cloned.1.call-done = bf16[32,2,32,2048]{3,2,1,0:T(8,128)(2,1)} async-done(((bf16[32,2,32,128]{3,2,1,0:T(8,128)(2,1)}), bf16[32,2,32,2048]{3,2,1,0:T(8,128)(2,1)}) %all-gather.2.cloned.1.call-update) | async-done | bytes 8388624 | tf_op jit(solution)/shard_map/all_gather | solution.py:118
  99.0 272.5 %while.16 = (s32[]{:T(128)}, f32[128,128]{0,1:T(8,128)S(1)}, s32[2,2048]{1,0:T(2,128)S(1)}, s32[128]{0:T(128)S(1)}, bf16[32,2,32,2048]{3,2,1,0:T(8,128)(2,1)}, /...) while((s32[]{:T(128)}, f32[128,128]{0,1:T(8,128)S(1)}, ...), condition=%wide.region_6.7_spmd, body=%wide.region_1.6_spmd.sunk | while | flops 197204160 | bytes 37496052 | solution.py:125
  99.2 1.8 convolution_bitcast_fusion.10
  101.5 1.7 copy-done
  105.1 1.4 convolution_bitcast_fusion.8
  112.5 1.8 convolution_bitcast_fusion.11
  116.2 1.8 convolution_bitcast_fusion.10
  118.5 1.7 copy-done
  129.5 1.8 convolution_bitcast_fusion.11
  133.3 1.8 convolution_bitcast_fusion.10
  135.6 1.7 copy-done
  139.1 1.4 convolution_bitcast_fusion.8
  146.5 1.8 convolution_bitcast_fusion.11
  150.3 1.8 convolution_bitcast_fusion.10
  152.6 1.7 copy-done
  163.6 1.8 convolution_bitcast_fusion.11
  167.3 1.8 convolution_bitcast_fusion.10
  169.6 1.7 copy-done
  173.2 1.4 convolution_bitcast_fusion.8
  180.6 1.8 convolution_bitcast_fusion.11
  184.4 1.8 convolution_bitcast_fusion.10
  186.7 1.7 copy-done
  190.2 1.4 convolution_bitcast_fusion.8
  197.6 1.8 convolution_bitcast_fusion.11
  201.4 1.8 convolution_bitcast_fusion.10
  203.7 1.7 copy-done
  207.3 1.4 convolution_bitcast_fusion.8
  214.7 1.8 convolution_bitcast_fusion.11
  218.4 1.8 convolution_bitcast_fusion.10
  220.7 1.7 copy-done
  224.3 1.4 convolution_bitcast_fusion.8
  231.7 1.8 convolution_bitcast_fusion.11
  235.5 1.8 convolution_bitcast_fusion.10
  237.8 1.7 copy-done
  241.4 1.4 convolution_bitcast_fusion.8
  248.7 1.8 convolution_bitcast_fusion.11
  252.5 1.8 convolution_bitcast_fusion.10
  254.8 1.7 copy-done
  265.8 1.8 convolution_bitcast_fusion.11
  269.5 1.8 convolution_bitcast_fusion.10
  271.8 1.7 copy-done
  282.8 1.8 convolution_bitcast_fusion.11
  286.6 1.8 convolution_bitcast_fusion.10
  288.9 1.7 copy-done
  299.9 1.8 convolution_bitcast_fusion.11
  303.6 1.8 convolution_bitcast_fusion.10
  305.9 1.7 copy-done
  316.9 1.8 convolution_bitcast_fusion.11
  320.6 1.8 convolution_bitcast_fusion.10
  323.0 1.7 copy-done
  333.9 1.8 convolution_bitcast_fusion.11
  337.7 1.8 convolution_bitcast_fusion.10
  340.0 1.7 copy-done
  351.0 1.8 convolution_bitcast_fusion.11
  354.7 1.8 convolution_bitcast_fusion.10
  357.0 1.7 copy-done
  368.0 1.8 convolution_bitcast_fusion.11
  372.5 69.3 %reduce-scatter.2.cloned.1.call-done = f32[1,16,128]{2,1,0:T(8,128)} async-done(((f32[16,16,128]{2,1,0:T(8,128)}), f32[1,16,128]{2,1,0:T(8,128)}) %reduce-scatter.2.cloned.1.call-update) | async-done | bytes 8208 | tf_op jit(solution)/shard_map/reduce_scatter | solution.py:137
  441.8 6.9 %all-to-all-start = ((f32[1,16,128]{2,0,1:T(1,128)}), f32[1,16,128]{2,0,1:T(1,128)S(1)}, u32[]{:S(2)}, u32[]{:S(2)}) async-start(f32[1,16,128]{2,0,1:T(1,128)} %bitcast.215), calls=%async_computation.1 | async-start | bytes 16384 | tf_op jit(solution)/shard_map/all_to_all | solution.py:138
  448.7 9.2 %cosine_multiply_fusion = (f32[512,1024]{1,0:T(8,128)S(1)}, f32[512,1024]{1,0:T(8,128)}) fusion(s32[1024]{0:T(1024)S(1)} %iota_add_fusion.4, f32[512]{0:T(512)S(1)} %get-tuple-element.288, f32[512]{0:T(512)S(1)} %get-tuple-element.289), kind=kLoop, calls=%fused_computation.207 | loop fusion | flops 8388608 | bytes 4202496 | tf_op jit(solution)/shard_map/mul | solution.py:18
  459.9 3.8 fusion.104
  463.7 2.1 fusion.103
  (716 shorter events, 140.8 us)
Async XLA Ops:
  7.2 1.9 copy-start.2
  7.2 91.8 %all-gather.2.cloned.1.call-start = ((), (), s32[]{:S(2)}) async-start(), calls=%async_computation.2 | async-start | bytes 8912896 | tf_op jit(solution)/shard_map/all_gather | solution.py:118
  7.9 433.9 %reduce-scatter.2.cloned.1.call-start = ((), (), s32[]{:S(2)}) async-start(), calls=%async_computation.3 | async-start | bytes 139264 | tf_op jit(solution)/shard_map/reduce_scatter | solution.py:137
  9.2 3.2 copy-start.4
  9.2 3.2 copy-start.3
  9.2 28.9 %copy-start.5 = (s32[128]{0:T(128)S(1)}, s32[128]{0:T(128)}, u32[]{:S(2)}) copy-start(s32[128]{0:T(128)} %param.9) | copy-start | bytes 1540
  101.0 2.2 copy-start
  118.0 2.2 copy-start
  135.0 2.2 copy-start
  152.1 2.2 copy-start
  169.1 2.2 copy-start
  186.2 2.2 copy-start
  203.2 2.2 copy-start
  220.2 2.2 copy-start
  237.3 2.2 copy-start
  254.3 2.2 copy-start
  271.3 2.2 copy-start
  288.4 2.2 copy-start
  305.4 2.2 copy-start
  322.4 2.2 copy-start
  339.5 2.2 copy-start
  356.5 2.2 copy-start
  441.8 16.1 %all-to-all-start = ((f32[1,16,128]{2,0,1:T(1,128)}), f32[1,16,128]{2,0,1:T(1,128)S(1)}, u32[]{:S(2)}, u32[]{:S(2)}) async-start(f32[1,16,128]{2,0,1:T(1,128)} %bitcast.215), calls=%async_computation.1 | async-start | bytes 16384 | tf_op jit(solution)/shard_map/all_to_all | solution.py:138
  459.9 3.8 copy-start.1
Sparse Core Ops, SparseCore 0:
  10.5 88.3 all-gather.1
  372.6 69.1 reduce-scatter.1
where the time goes:
time: 482 us; the launch traced here: 476 us
  matrix products  136 us (28%)
  waiting for transfers between devices  131 us (27%)
  other arithmetic  59.5 us (12%)
  local copies, waits for them, and re-layouts  56 us (12%)
  loops' own time  45.8 us (10%)
  blocking collectives  25.7 us (5%)
  between operations  15.6 us (3%)
  starting transfers between devices  6.94 us (1%)
    dot_general x64, matrix products, accumulate(): jnp.einsum('fkpsa,fpsb->fkab', left_side[..., first_row:first_row + row_c...  102 us
    reduce_scatter x1, waiting for transfers between devices, on_device(): shares = lax.psum_scatter(packed, 'loop', scatter_dimension=0, tiled=True)  69.3 us
    all_gather x1, waiting for transfers between devices, on_device(): block_in = lax.all_gather(spectra, 'loop', axis=3, tiled=True)  60.7 us
    another operation x1, loops' own time, on_device(): running = lax.fori_loop(0, shard_count, one_shard, empty_sum)  45.8 us
    dot_general x64, matrix products, accumulate(): lax.dot_general(components, onehot, (((1,), (1,)), ((), ())), preferred_e...  27.7 us
    while x32, local copies, waits for them, and re-layouts  26.8 us
    all_gather x1, blocking collectives, on_device(): lax.all_gather(jnp.stack([channel_loc, channel_valid]), 'loop', axis=1, t...  25.7 us
    another operation x64, other arithmetic  20.4 us
  transfers between devices with their start and end apart: 3, of which 2 were waited for; matrix products, arithmetic and copies ran while one was open for 3% of the time, Pallas kernels for 0%

commit v1 on v0

v1 whole, which is shorter than its diff:
```python
import math

import jax
import jax.numpy as jnp
from jax import lax
from jax.experimental import pallas as pl
from jax.experimental.pallas import tpu as pltpu
from jax.sharding import PartitionSpec as P

BCAP = 16
F32 = jnp.float32
BF16 = jnp.bfloat16


def iota(shape, dim):
    return lax.broadcasted_iota(jnp.int32, shape, dim)


def dot_nt(a, b):
    return lax.dot_general(a, b, (((1,), (1,)), ((), ())), preferred_element_type=F32)


def dot_nn(a, b):
    return lax.dot_general(a, b, (((1,), (0,)), ((), ())), preferred_element_type=F32)


def pack_kernel(loc_ref, valid_ref, x_ref, o_ref):
    row = iota((128, 128), 0)
    col = iota((128, 128), 1)
    valid = jnp.broadcast_to(valid_ref[...].astype(F32), (128, 128))
    pick = jnp.where(col == 16 * (row % 8) + row // 8, valid, 0.0).astype(BF16)
    jit = jnp.broadcast_to((loc_ref[...] & 1).astype(F32), (16, 128))
    jit = jnp.where(iota((16, 128), 1) % 16 == iota((16, 128), 0), jit, 0.0).astype(BF16)
    spread = jnp.where(col == row // 16, 1.0, 0.0).astype(BF16)
    bits = dot_nn(jit, spread).astype(BF16)
    for g in range(x_ref.shape[0]):
        o_ref[g, 0:128] = dot_nt(pick, x_ref[g]).astype(BF16)
        o_ref[g, 128:144] = bits


def pack(channel_loc, channel_valid, blocks):
    count = blocks.shape[0]
    step = 4
    return pl.pallas_call(
        pack_kernel,
        grid=(count // step,),
        in_specs=[
            pl.BlockSpec((1, 128), lambda i: (0, 0)),
            pl.BlockSpec((1, 128), lambda i: (0, 0)),
            pl.BlockSpec((step, 128, 128), lambda i: (i, 0, 0)),
        ],
        out_specs=pl.BlockSpec((step, 144, 128), lambda i: (i, 0, 0)),
        out_shape=jax.ShapeDtypeStruct((count, 144, 128), BF16),
        name="pack",
    )(channel_loc.reshape(1, 128), channel_valid.reshape(1, 128), blocks)


def split3(x):
    hi = x.astype(BF16)
    rest = x - hi.astype(F32)
    mid = rest.astype(BF16)
    low = (rest - mid.astype(F32)).astype(BF16)
    return hi, mid, low


def skew_sum(x):
    total = x[0:8]
    for g in range(1, 16):
        total = total + pltpu.roll(x[8 * g : 8 * g + 8], 128 - 8 * g, 1)
    out = total[0:1]
    for s in range(1, 8):
        out = out + pltpu.roll(total[s : s + 1], 128 - s, 1)
    return out


CHUNK = 64
NCHUNK = 128 // CHUNK


def main_kernel(owner_row_ref, owner_col_ref, y_ref, o_ref, x_s, w_s, lin_s, acc_s, bits_s, pw_s):
    lane = iota((128, 128), 1)
    row = iota((128, 128), 0)
    sign = jnp.where(row // 32 % 2 == 1, 1.0, -1.0)
    swap = jnp.where(row == jnp.where(lane // 32 % 2 == 0, lane + 32, lane - 32), sign, 0.0).astype(BF16)

    bits = jnp.zeros((16, 128), F32)
    for g in range(16):
        piece = y_ref[g, 128:144, :].astype(F32)
        bits = bits + (pltpu.roll(piece, 8 * g, 1) if g else piece)
    bits_s[...] = bits
    bits_t = jnp.transpose(jnp.concatenate([bits, jnp.zeros((112, 128), F32)], 0))

    suffix = jnp.zeros((128, 128), F32)
    for r in reversed(range(16)):
        x = y_ref[:, 8 * r : 8 * r + 8, :].astype(F32).reshape(128, 128)
        xb = x.astype(BF16)
        for c in range(NCHUNK):
            x_s[c, CHUNK * r : CHUNK * r + CHUNK, :] = xb[CHUNK * c : CHUNK * c + CHUNK]
        xs = dot_nn(xb, swap)
        for f in range(2):
            mine = lane // 64 == f
            w_s[f, r, 0:128, :] = jnp.where(mine, x, 0.0).astype(BF16)
            w_s[f, r, 128:256, :] = jnp.where(mine, xs, 0.0).astype(BF16)
        hi = suffix.astype(BF16)
        lin_s[r, :, 0:128] = hi
        lin_s[r, :, 128:256] = (suffix - hi.astype(F32)).astype(BF16)
        suffix = suffix + x

    keep_low = row > lane
    keep_diag = row >= lane

    def one_freq(f, carry):
        lin = jnp.zeros((128, 256), F32)
        lin_same = jnp.zeros((128, 256), F32)
        lin_jit = jnp.zeros((128, 256), F32)
        acc_s[...] = jnp.zeros(acc_s.shape, F32)
        for r in range(16):
            w = w_s[f, r]
            lin = lin + dot_nt(lin_s[r], jnp.concatenate([w, w], 1))
            jit_lane = jnp.broadcast_to(bits_s[r : r + 1, :], (CHUNK, 128))
            for c in range(NCHUNK):
                rows = slice(CHUNK * c, CHUNK * c + CHUNK)
                prod = dot_nt(x_s[c, CHUNK * r :, :], w)
                acc_re = None
                for u in range(r, 16):
                    at = CHUNK * (u - r)
                    re = prod[at : at + CHUNK, 0:128]
                    im = prod[at : at + CHUNK, 128:256]
                    gain = lax.rsqrt(jnp.maximum(re * re + im * im, 1.0))
                    pr = re * gain
                    pi = im * gain
                    if u == r:
                        mask = jit_lane * (1.0 - jnp.broadcast_to(bits_t[rows, r : r + 1], (CHUNK, 128)))
                        acc_s[1, rows, 0:128] += pr
                        acc_s[1, rows, 128:256] += pi
                        acc_s[2, rows, 0:128] += pr * mask
                        acc_s[2, rows, 128:256] += pi * mask
                        acc_s[3, rows, 0:128] += re
                        acc_s[3, rows, 128:256] += im
                        acc_s[4, rows, 0:128] += re * mask
                        acc_s[4, rows, 128:256] += im * mask
                    elif acc_re is None:
                        acc_re, acc_im = pr, pi
                    else:
                        acc_re = acc_re + pr
                        acc_im = acc_im + pi
                if acc_re is not None:
                    acc_s[0, rows, 0:128] += acc_re
                    acc_s[0, rows, 128:256] += acc_im
        for part in range(4):
            cols = slice(128 * (part % 2), 128 * (part % 2) + 128)
            conj = 1.0 if part % 2 == 0 else -1.0
            if part < 2:
                full, same, jit = lin[:, cols], acc_s[3, :, cols], acc_s[4, :, cols]
            else:
                full, same, jit = acc_s[0, :, cols], acc_s[1, :, cols], acc_s[2, :, cols]
            low = jnp.where(keep_diag, full, 0.0) + jnp.where(keep_low, same - jit, 0.0)
            up = jnp.where(keep_diag, 0.0, full * conj)
            up = up + jnp.transpose(jnp.where(keep_low, jit, 0.0))
            pw_s[f, part : part + 1, 0:128] = skew_sum(low)
            pw_s[f, part : part + 1, 128:256] = skew_sum(up)
        return carry

    pw_s[...] = jnp.zeros(pw_s.shape, F32)
    lax.fori_loop(0, 2, one_freq, 0)

    owner_row = jnp.broadcast_to(owner_row_ref[...], (128, 128))
    owner_col = jnp.broadcast_to(owner_col_ref[...], (128, 128))
    before = jnp.where((owner_row == owner_col) & (lane < row), 1.0, 0.0)
    rank = jnp.sum(before, 1, keepdims=True).astype(jnp.int32)
    slot = jnp.broadcast_to(16 * owner_col_ref[...] + rank, (128, 256))
    place = jnp.where(slot == iota((128, 256), 1), 1.0, 0.0)
    low_pick = jnp.where((lane + row) % 128 == 0, 1.0, 0.0).astype(BF16)
    up_pick = jnp.where(row == lane + 1, 1.0, 0.0).astype(BF16)
    unpick = jnp.concatenate([low_pick, up_pick], 0)
    place_b = place.astype(BF16)
    gather = dot_nn(unpick, place_b).astype(BF16)
    hi, mid, low = split3(pw_s[...].reshape(16, 256))
    sums = dot_nn(hi, gather) + dot_nn(mid, gather) + dot_nn(low, gather)
    out = []
    for f in range(2):
        part = [sums[8 * f + p : 8 * f + p + 1] for p in range(4)]
        power = part[2] * part[2] + part[3] * part[3]
        out += [part[0], part[1], part[0] * power, part[1] * power]
    o_ref[...] = jnp.concatenate(out, 0)


def bin_sums(bin_owner, received):
    return pl.pallas_call(
        main_kernel,
        out_shape=jax.ShapeDtypeStruct((8, 256), F32),
        scratch_shapes=[
            pltpu.VMEM((NCHUNK, 16 * CHUNK, 128), BF16),
            pltpu.VMEM((2, 16, 256, 128), BF16),
            pltpu.VMEM((16, 128, 256), BF16),
            pltpu.VMEM((5, 128, 256), F32),
            pltpu.VMEM((16, 128), F32),
            pltpu.VMEM((2, 8, 256), F32),
        ],
        name="bin_sums",
    )(bin_owner.reshape(1, 128), bin_owner.reshape(128, 1), received)


def on_device(spectra, channel_loc, channel_valid, bin_owner):
    groups = lax.axis_size("loop")
    owners = lax.axis_size("stack")
    blocks = spectra.reshape(groups, 128, 128)
    packed = pack(channel_loc, channel_valid, blocks)
    received = lax.all_to_all(packed, "loop", split_axis=0, concat_axis=0, tiled=True)
    sums = bin_sums(bin_owner, received)
    by_rank = sums.reshape(8, owners, BCAP).transpose(2, 1, 0).reshape(BCAP, owners * 8)
    by_rank = lax.all_to_all(by_rank, "loop", split_axis=0, concat_axis=0, tiled=True)
    by_owner = by_rank.reshape(groups, owners, 8).transpose(1, 0, 2).reshape(owners, groups * 8)
    mine = lax.all_to_all(by_owner, "stack", split_axis=0, concat_axis=0, tiled=True)
    mine = mine.reshape(owners * groups * 2, 4).T
    return finish(mine)


def finish(mine):
    return finish_plain(mine)


def lag_matrix(freq_count):
    freq_ids = jnp.arange(freq_count, dtype=jnp.int32)
    lag_ids = jnp.arange(2 * freq_count, dtype=jnp.int32) - freq_count
    turn_count = freq_ids[:, None] * lag_ids[None, :] % (2 * freq_count)
    phase_angle = turn_count.astype(jnp.float32) * (math.pi / freq_count)
    bin_weight = jnp.where(freq_ids == 0, 1.0, 2.0).astype(jnp.float32)[:, None]
    return jnp.concatenate(
        [bin_weight * jnp.cos(phase_angle), -bin_weight * jnp.sin(phase_angle)], 0
    )


def normalize(series):
    return series / jnp.sqrt(jnp.mean(series * series, axis=-1, keepdims=True) + 1e-06)


def finish_plain(mine):
    both = mine.reshape(2, -1)
    series = jnp.dot(both, lag_matrix(mine.shape[1]), precision=lax.Precision.HIGHEST)
    series = normalize(series)
    return series[0].reshape(1, 1, -1), series[1].reshape(1, 1, -1)


def solution(mesh):
    in_specs = (P("stack", None, None, "loop"), P("loop"), P("loop"), P())
    out_specs = (P("stack", "loop", None), P("stack", "loop", None))
    return jax.shard_map(
        on_device, mesh=mesh, in_specs=in_specs, out_specs=out_specs, check_vma=False
    )
```

time: 482 us -> 74.1 us (0.15); the launches traced: 476 us -> 73.6 us
  matrix products: 136 us -> 3.79 us
  waiting for transfers between devices: 131 us -> 18 us
  local copies, waits for them, and re-layouts: 56 us -> 5.4 us
  other arithmetic: 59.5 us -> 9.97 us
  loops' own time: 45.8 us -> 0 us
  blocking collectives: 25.7 us -> 0 us
  between operations: 15.6 us -> 0.7 us
  starting transfers between devices: 6.94 us -> 21.6 us
  Pallas kernels: 0 us -> 14.2 us
    dot_general x131 -> x1, matrix products: 136 us -> 3.79 us  [finish_plain(): jnp.dot(both, lag_matrix(mine.shape[1]), precision=lax.Precision.HIGHEST)]
    reduce_scatter x1 -> x0, waiting for transfers between devices: 69.3 us -> none  [on_device(): shares = lax.psum_scatter(packed, 'loop', scatter_dimension=0, tiled=True)]
    all_gather x1 -> x0, waiting for transfers between devices: 60.7 us -> none  [on_device(): block_in = lax.all_gather(spectra, 'loop', axis=3, tiled=True)]
    another operation x1 -> x0, loops' own time: 45.8 us -> none  [on_device(): running = lax.fori_loop(0, shard_count, one_shard, empty_sum)]
    while x33 -> x0, local copies, waits for them, and re-layouts: 29.9 us -> none
    another operation x131 -> x0, other arithmetic: 28.8 us -> none
    all_gather x1 -> x0, blocking collectives: 25.7 us -> none  [on_device(): lax.all_gather(jnp.stack([channel_loc, channel_valid]), 'loop', axis=1, t...]
    all_to_all x1 -> x3, waiting for transfers between devices: 0.01 us -> 18 us  [the longest x1 10.9 us: on_device(): lax.all_to_all(packed, 'loop', split_axis=0, concat_axis=0, tiled=True)]
  transfers between devices with their start and end apart: 3 -> 3, of which waited for: 2 -> 2; matrix products, arithmetic and copies ran while one was open for 3% -> 14% of each run, Pallas kernels for 0% -> 0%
where the time goes in v1:
time: 74.1 us; the launch traced here: 73.6 us
  starting transfers between devices  21.6 us (29%)
  waiting for transfers between devices  18 us (24%)
  Pallas kernels  14.2 us (19%)
  other arithmetic  9.97 us (13%)
  local copies, waits for them, and re-layouts  5.4 us (7%)
  matrix products  3.79 us (5%)
    all_to_all x1, waiting for transfers between devices, on_device(): lax.all_to_all(packed, 'loop', split_axis=0, concat_axis=0, tiled=True)  10.9 us
    pallas_call x1, Pallas kernels, bin_sums(): pl.pallas_call(main_kernel, out_shape=jax.ShapeDtypeStruct((8, 256), F32)...  10.6 us
    mul x1, other arithmetic, lag_matrix(): bin_weight * jnp.cos(phase_angle)  9.21 us
    all_to_all x1, starting transfers between devices, on_device(): lax.all_to_all(packed, 'loop', split_axis=0, concat_axis=0, tiled=True)  8.44 us
    all_to_all x1, starting transfers between devices, on_device(): lax.all_to_all(by_owner, 'stack', split_axis=0, concat_axis=0, tiled=True)  8.4 us
    all_to_all x1, waiting for transfers between devices, on_device(): lax.all_to_all(by_rank, 'loop', split_axis=0, concat_axis=0, tiled=True)  7.07 us
    all_to_all x1, starting transfers between devices, on_device(): lax.all_to_all(by_rank, 'loop', split_axis=0, concat_axis=0, tiled=True)  4.77 us
    dot_general x1, matrix products, finish_plain(): jnp.dot(both, lag_matrix(mine.shape[1]), precision=lax.Precision.HIGHEST)  3.79 us
  transfers between devices with their start and end apart: 3, of which 2 were waited for; matrix products, arithmetic and copies ran while one was open for 14% of the time, Pallas kernels for 0%

profile of v1, /device:TPU:1, one launch (start us, length us, event | category | flops | bytes accessed | tf_op | source)
XLA Modules:
  0.0 73.6 jit_solution(11715704093953963489)
XLA Ops:
  0.6 0.0 copy-start.1
  0.6 3.6 %pack.1 = bf16[16,144,128]{2,1,0:T(8,128)(2,1)} custom-call(s32[1,128]{1,0:T(1,128)} %bitcast.27, s32[1,128]{1,0:T(1,128)} %bitcast.28, bf16[16,128,128]{2,1,0:T(8,128)(2,1)} %bitcast.21), custom_call_target="tpu_custom_call" | custom-call | tf_op jit(solution)/shard_map/pack/pallas_call | solution.py:44
  4.2 8.4 %all-to-all-start = ((bf16[16,144,128]{2,1,0:T(8,128)(2,1)}), bf16[16,144,128]{2,1,0:T(8,128)(2,1)S(1)}, u32[]{:S(2)}, u32[]{:S(2)}) async-start(bf16[16,144,128]{2,1,0:T(8,128)(2,1)} %pack.1), calls=%async_computation | async-start | bytes 1179648 | tf_op jit(solution)/shard_map/all_to_all | solution.py:209
  12.7 0.0 copy-done.1
  12.7 0.7 copy.12.owner_col_ref
  13.4 10.9 %all-to-all-done.y_ref = bf16[16,144,128]{2,1,0:T(8,128)(2,1)S(1)} async-done(((bf16[16,144,128]{2,1,0:T(8,128)(2,1)}), bf16[16,144,128]{2,1,0:T(8,128)(2,1)S(1)}, u32[]{:S(2)}, u32[]{:S(2)}) %all-to-all-start) | async-done | bytes 589856 | tf_op jit(solution)/shard_map/all_to_all | solution.py:209
  24.3 0.0 copy-start
  24.3 0.8 %copy-done = bf16[16,144,128]{2,1,0:T(8,128)(2,1)} copy-done((bf16[16,144,128]{2,1,0:T(8,128)(2,1)}, bf16[16,144,128]{2,1,0:T(8,128)(2,1)S(1)}, u32[]{:S(2)}) %copy-start) | copy-done | bytes 589848
  25.1 10.6 %bin_sums.1 = f32[8,256]{1,0:T(8,128)} custom-call(s32[1,128]{1,0:T(1,128)} %bitcast.25, s32[128,1]{1,0:T(8,128)} %copy.12.owner_col_ref, bf16[16,144,128]{2,1,0:T(8,128)(2,1)} %copy-done), custom_call_target="tpu_custom_call" | custom-call | tf_op jit(solution)/shard_map/bin_sums/pallas_call | solution.py:189
  35.8 0.8 %reshape.67 = f32[8,16,16]{2,1,0:T(8,128)S(1)} reshape(f32[8,256]{1,0:T(8,128)} %bin_sums.1) | data formatting | bytes 16384 | tf_op jit(solution)/shard_map/reshape | solution.py:211
  36.6 0.7 copy.14
  37.2 4.8 %all-to-all-start.1 = ((f32[16,1,128]{2,1,0:T(1,128)}), f32[16,1,128]{2,1,0:T(1,128)S(1)}, u32[]{:S(2)}, u32[]{:S(2)}) async-start(f32[16,1,128]{2,1,0:T(1,128)} %copy.14), calls=%async_computation.1 | async-start | bytes 16384 | tf_op jit(solution)/shard_map/all_to_all | solution.py:212
  42.0 7.1 %all-to-all-done.1 = f32[16,1,128]{2,1,0:T(1,128)S(1)} async-done(((f32[16,1,128]{2,1,0:T(1,128)}), f32[16,1,128]{2,1,0:T(1,128)S(1)}, u32[]{:S(2)}, u32[]{:S(2)}) %all-to-all-start.1) | async-done | bytes 8224 | tf_op jit(solution)/shard_map/all_to_all | solution.py:212
  49.1 0.1 copy.15
  49.2 0.1 copy.16
  49.3 0.7 copy.17
  49.9 8.4 %all-to-all-start.2 = ((f32[16,1,128]{2,1,0:T(1,128)}), f32[16,1,128]{2,1,0:T(1,128)S(1)}, u32[]{:S(2)}, u32[]{:S(2)}) async-start(f32[16,1,128]{2,1,0:T(1,128)} %copy.17), calls=%async_computation.2 | async-start | bytes 16384 | tf_op jit(solution)/shard_map/all_to_all | solution.py:214
  58.3 9.2 %cosine_multiply_fusion = (f32[512,1024]{1,0:T(8,128)S(1)}, f32[512,1024]{1,0:T(8,128)}) fusion(s32[1024]{0:T(1024)S(1)} %iota_add_fusion, f32[512]{0:T(512)S(1)} %get-tuple-element.8, f32[512]{0:T(512)S(1)} %get-tuple-element.9), kind=kLoop, calls=%fused_computation.11 | loop fusion | flops 8388608 | bytes 4202496 | tf_op jit(solution)/shard_map/mul | solution.py:230
  67.6 0.0 all-to-all-done.2
  67.6 0.5 broadcast.66
  68.1 0.7 reduce.3
  68.7 0.3 reshape.69
  69.0 0.1 copy.18
  69.2 3.8 %multiply_reduce_fusion = (f32[2]{0:T(128)S(1)}, f32[2,1024]{1,0:T(2,128)S(1)}) fusion(f32[2,1024]{1,0:T(2,128)S(1)} %reshape.70, f32[512,1024]{1,0:T(8,128)} %get-tuple-element.5, f32[512,1024]{1,0:T(8,128)S(1)} %get-tuple-element.4), kind=kOutput, calls=%fused_computation.16 | convolution fusion | flops 26218494 | bytes 4210696 | tf_op jit(solution)/shard_map/dot_general | solution.py:240
  73.0 0.1 broadcast_divide_fusion
  73.0 0.6 slice_bitcast_fusion
  (5 shorter events, 0.1 us)
Async XLA Ops:
  0.6 12.0 %copy-start.1 = (s32[128]{0:T(128)S(1)}, s32[128]{0:T(128)}, u32[]{:S(2)}) copy-start(s32[128]{0:T(128)} %param.7) | copy-start | bytes 1540
  4.2 20.1 %all-to-all-start = ((bf16[16,144,128]{2,1,0:T(8,128)(2,1)}), bf16[16,144,128]{2,1,0:T(8,128)(2,1)S(1)}, u32[]{:S(2)}, u32[]{:S(2)}) async-start(bf16[16,144,128]{2,1,0:T(8,128)(2,1)} %pack.1), calls=%async_computation | async-start | bytes 1179648 | tf_op jit(solution)/shard_map/all_to_all | solution.py:209
  24.3 0.8 %copy-start = (bf16[16,144,128]{2,1,0:T(8,128)(2,1)}, bf16[16,144,128]{2,1,0:T(8,128)(2,1)S(1)}, u32[]{:S(2)}) copy-start(bf16[16,144,128]{2,1,0:T(8,128)(2,1)S(1)} %all-to-all-done.y_ref) | copy-start | bytes 1769476
  37.2 11.8 %all-to-all-start.1 = ((f32[16,1,128]{2,1,0:T(1,128)}), f32[16,1,128]{2,1,0:T(1,128)S(1)}, u32[]{:S(2)}, u32[]{:S(2)}) async-start(f32[16,1,128]{2,1,0:T(1,128)} %copy.14), calls=%async_computation.1 | async-start | bytes 16384 | tf_op jit(solution)/shard_map/all_to_all | solution.py:212
  49.9 17.6 %all-to-all-start.2 = ((f32[16,1,128]{2,1,0:T(1,128)}), f32[16,1,128]{2,1,0:T(1,128)S(1)}, u32[]{:S(2)}, u32[]{:S(2)}) async-start(f32[16,1,128]{2,1,0:T(1,128)} %copy.17), calls=%async_computation.2 | async-start | bytes 16384 | tf_op jit(solution)/shard_map/all_to_all | solution.py:214

commit v2 on v1

--- a/solution.py
+++ b/solution.py
@@ -1,13 +1,11 @@
-import math
-
 import jax
 import jax.numpy as jnp
+import numpy as np
 from jax import lax
 from jax.experimental import pallas as pl
 from jax.experimental.pallas import tpu as pltpu
 from jax.sharding import PartitionSpec as P
 
-BCAP = 16
 F32 = jnp.float32
 BF16 = jnp.bfloat16
 
@@ -73,11 +71,16 @@
     return out
 
 
+def exact_dot(x, picks):
+    hi, mid, rest = split3(x)
+    return dot_nn(hi, picks) + dot_nn(mid, picks) + dot_nn(rest, picks)
+
+
 CHUNK = 64
 NCHUNK = 128 // CHUNK
 
 
-def main_kernel(owner_row_ref, owner_col_ref, y_ref, o_ref, x_s, w_s, lin_s, acc_s, bits_s, pw_s):
+def main_kernel(owner_row_ref, y_ref, o_ref, x_s, w_s, lin_s, acc_s, bits_s, pw_s):
     lane = iota((128, 128), 1)
     row = iota((128, 128), 0)
     sign = jnp.where(row // 32 % 2 == 1, 1.0, -1.0)
@@ -164,31 +167,33 @@
     pw_s[...] = jnp.zeros(pw_s.shape, F32)
     lax.fori_loop(0, 2, one_freq, 0)
 
-    owner_row = jnp.broadcast_to(owner_row_ref[...], (128, 128))
-    owner_col = jnp.broadcast_to(owner_col_ref[...], (128, 128))
-    before = jnp.where((owner_row == owner_col) & (lane < row), 1.0, 0.0)
-    rank = jnp.sum(before, 1, keepdims=True).astype(jnp.int32)
-    slot = jnp.broadcast_to(16 * owner_col_ref[...] + rank, (128, 256))
-    place = jnp.where(slot == iota((128, 256), 1), 1.0, 0.0)
-    low_pick = jnp.where((lane + row) % 128 == 0, 1.0, 0.0).astype(BF16)
-    up_pick = jnp.where(row == lane + 1, 1.0, 0.0).astype(BF16)
-    unpick = jnp.concatenate([low_pick, up_pick], 0)
-    place_b = place.astype(BF16)
-    gather = dot_nn(unpick, place_b).astype(BF16)
-    hi, mid, low = split3(pw_s[...].reshape(16, 256))
-    sums = dot_nn(hi, gather) + dot_nn(mid, gather) + dot_nn(low, gather)
+    low_pick = jnp.where((lane + row) % 128 == 0, 1.0, 0.0)
+    up_pick = jnp.where(row == lane + 1, 1.0, 0.0)
+    unpick = jnp.concatenate([low_pick, up_pick], 0).astype(BF16)
+    sums = exact_dot(pw_s[...].reshape(16, 256), unpick)
     out = []
     for f in range(2):
         part = [sums[8 * f + p : 8 * f + p + 1] for p in range(4)]
         power = part[2] * part[2] + part[3] * part[3]
         out += [part[0], part[1], part[0] * power, part[1] * power]
-    o_ref[...] = jnp.concatenate(out, 0)
+    owner_row = jnp.broadcast_to(owner_row_ref[...], (128, 128))
+    earlier = (owner_row == jnp.transpose(owner_row)) & (row < lane)
+    rank = jnp.sum(jnp.where(earlier, 1.0, 0.0), 0, keepdims=True).astype(jnp.int32)
+    slot = 16 * owner_row_ref[...] + rank
+    place = jnp.where(iota((256, 128), 0) == slot, 1.0, 0.0).astype(BF16)
+    by_bin = jnp.transpose(jnp.concatenate(out + [jnp.zeros((120, 128), F32)], 0))
+    hi, mid, rest = split3(by_bin)
+    placed = dot_nn(place, hi) + dot_nn(place, mid) + dot_nn(place, rest)
+    o_ref[...] = placed[:, 0:8]
 
 
 def bin_sums(bin_owner, received):
+    vmem = pl.BlockSpec(memory_space=pltpu.VMEM)
     return pl.pallas_call(
         main_kernel,
-        out_shape=jax.ShapeDtypeStruct((8, 256), F32),
+        in_specs=[vmem, vmem],
+        out_specs=vmem,
+        out_shape=jax.ShapeDtypeStruct((256, 8), F32),
         scratch_shapes=[
             pltpu.VMEM((NCHUNK, 16 * CHUNK, 128), BF16),
             pltpu.VMEM((2, 16, 256, 128), BF16),
@@ -198,48 +203,67 @@
             pltpu.VMEM((2, 8, 256), F32),
         ],
         name="bin_sums",
-    )(bin_owner.reshape(1, 128), bin_owner.reshape(128, 1), received)
+    )(bin_owner.reshape(1, 128), received)
+
+
+def lag_tables():
+    lane = np.arange(128)
+    f0 = lane // 8 * 2 + lane % 8 // 4
+    imag = lane % 2
+    weight = np.full((16, 128), 2.0) * np.where(f0 % 2, -1.0, 1.0)
+    weight[0, f0 == 0] = 1.0
+    turn0 = 2 * np.pi * (np.arange(32)[:, None] * np.arange(16) % 32) / 32
+    first = np.concatenate([np.cos(turn0), np.sin(turn0)], 0)
+    turn1 = 2 * np.pi * (np.arange(128)[:, None] * f0 % 1024) / 1024
+    t1 = np.where(imag, -np.sin(turn1), np.cos(turn1))
+    t2 = np.where(imag, -np.cos(turn1), -np.sin(turn1))
+    turn2 = 2 * np.pi * (np.arange(8)[:, None] * f0 % 8) / 8
+    which = [lane % 4 // 2 == 0, lane % 4 // 2 == 1]
+    last = [np.concatenate([np.cos(turn2) * w, -np.sin(turn2) * w], 1) for w in which]
+    return [np.asarray(t, np.float32) for t in (weight, first, np.stack([t1, t2]), np.concatenate(last, 0))]
+
+
+def finish_kernel(x_ref, weight_ref, first_ref, twiddle_ref, last_ref, lin_ref, phase_ref):
+    spread = jnp.where(iota((8, 128), 0) == iota((8, 128), 1) % 8, 1.0, 0.0).astype(BF16)
+    wide = exact_dot(x_ref[...], spread)
+    wide = jnp.where(iota((256, 128), 0) % 16 == iota((256, 128), 1) // 8, wide, 0.0)
+    z = jnp.sum(wide.reshape(16, 16, 128), 1) * weight_ref[...]
+    high = lax.Precision.HIGHEST
+    v = jnp.dot(first_ref[...], z, precision=high, preferred_element_type=F32)
+    g = jnp.concatenate([v[0:32]] * 4, 0)
+    h = jnp.concatenate([v[32:64]] * 4, 0)
+    t1 = twiddle_ref[0]
+    t2 = twiddle_ref[1]
+    q = jnp.concatenate([g * t1 + h * t2, h * t1 - g * t2], 1)
+    series = lax.dot_general(
+        last_ref[...], q, (((1,), (1,)), ((), ())), precision=high, preferred_element_type=F32
+    )
+    for i, o_ref in enumerate((lin_ref, phase_ref)):
+        c = series[8 * i : 8 * i + 8]
+        o_ref[...] = c / jnp.sqrt(jnp.sum(c * c) * (1.0 / 1024) + 1e-06)
+
+
+def finish(mine):
+    vmem = pl.BlockSpec(memory_space=pltpu.VMEM)
+    return pl.pallas_call(
+        finish_kernel,
+        in_specs=[vmem] * 5,
+        out_specs=[vmem] * 2,
+        out_shape=[jax.ShapeDtypeStruct((8, 128), F32)] * 2,
+        name="finish",
+    )(mine, *[jnp.asarray(t) for t in lag_tables()])
+
+
+def exchange(x, axis):
+    return lax.all_to_all(x, axis, split_axis=0, concat_axis=0, tiled=True)
 
 
 def on_device(spectra, channel_loc, channel_valid, bin_owner):
-    groups = lax.axis_size("loop")
-    owners = lax.axis_size("stack")
-    blocks = spectra.reshape(groups, 128, 128)
-    packed = pack(channel_loc, channel_valid, blocks)
-    received = lax.all_to_all(packed, "loop", split_axis=0, concat_axis=0, tiled=True)
+    blocks = spectra.reshape(lax.axis_size("loop"), 128, 128)
+    received = exchange(pack(channel_loc, channel_valid, blocks), "loop")
     sums = bin_sums(bin_owner, received)
-    by_rank = sums.reshape(8, owners, BCAP).transpose(2, 1, 0).reshape(BCAP, owners * 8)
-    by_rank = lax.all_to_all(by_rank, "loop", split_axis=0, concat_axis=0, tiled=True)
-    by_owner = by_rank.reshape(groups, owners, 8).transpose(1, 0, 2).reshape(owners, groups * 8)
-    mine = lax.all_to_all(by_owner, "stack", split_axis=0, concat_axis=0, tiled=True)
-    mine = mine.reshape(owners * groups * 2, 4).T
-    return finish(mine)
-
-
-def finish(mine):
-    return finish_plain(mine)
-
-
-def lag_matrix(freq_count):
-    freq_ids = jnp.arange(freq_count, dtype=jnp.int32)
-    lag_ids = jnp.arange(2 * freq_count, dtype=jnp.int32) - freq_count
-    turn_count = freq_ids[:, None] * lag_ids[None, :] % (2 * freq_count)
-    phase_angle = turn_count.astype(jnp.float32) * (math.pi / freq_count)
-    bin_weight = jnp.where(freq_ids == 0, 1.0, 2.0).astype(jnp.float32)[:, None]
-    return jnp.concatenate(
-        [bin_weight * jnp.cos(phase_angle), -bin_weight * jnp.sin(phase_angle)], 0
-    )
-
-
-def normalize(series):
-    return series / jnp.sqrt(jnp.mean(series * series, axis=-1, keepdims=True) + 1e-06)
-
-
-def finish_plain(mine):
-    both = mine.reshape(2, -1)
-    series = jnp.dot(both, lag_matrix(mine.shape[1]), precision=lax.Precision.HIGHEST)
-    series = normalize(series)
-    return series[0].reshape(1, 1, -1), series[1].reshape(1, 1, -1)
+    linear, phase = finish(exchange(sums, ("stack", "loop")))
+    return linear.reshape(1, 1, -1), phase.reshape(1, 1, -1)
 
 
 def solution(mesh):

time: 74.1 us -> 62 us (0.84)
  blocking collectives: 0 us -> 44.6 us
  starting transfers between devices: 21.6 us -> 0 us
  waiting for transfers between devices: 18 us -> 0 us
  other arithmetic: 9.97 us -> 0 us
  local copies, waits for them, and re-layouts: 5.4 us -> 0 us
  matrix products: 3.79 us -> 0 us
  Pallas kernels: 14.2 us -> 16.5 us
    all_to_all x0 -> x2, blocking collectives: none -> 44.6 us  [exchange(): return lax.all_to_all(x, axis, split_axis=0, concat_axis=0, tiled=True)]
    all_to_all x3 -> x0, starting transfers between devices: 21.6 us -> none  [the longest x1 8.44 us: on_device(): lax.all_to_all(packed, 'loop', split_axis=0, concat_axis=0, tiled=True)]
    all_to_all x3 -> x0, waiting for transfers between devices: 18 us -> none  [the longest x1 10.9 us: on_device(): lax.all_to_all(packed, 'loop', split_axis=0, concat_axis=0, tiled=True)]
    mul x1 -> x0, other arithmetic: 9.21 us -> none  [lag_matrix(): bin_weight * jnp.cos(phase_angle)]
    dot_general x1 -> x0, matrix products: 3.79 us -> none  [finish_plain(): jnp.dot(both, lag_matrix(mine.shape[1]), precision=lax.Precision.HIGHEST)]
    pallas_call x1 -> x2, Pallas kernels: 10.6 us -> 12.9 us  [the longest x1 10.5 us: bin_sums(): pl.pallas_call(main_kernel, in_specs=[vmem, vmem], out_specs=vmem, out_sh...]
    all_to_all x4 -> x0, local copies, waits for them, and re-layouts: 1.94 us -> none  [the longest x2 1.17 us: on_device(): lax.all_to_all(by_owner, 'stack', split_axis=0, concat_axis=0, tiled=True)]
    reshape x5 -> x0, local copies, waits for them, and re-layouts: 1.81 us -> none  [the longest x2 0.8 us: on_device(): sums.reshape(8, owners, BCAP).transpose(2, 1, 0).reshape(BCAP, owners * 8)]
  transfers between devices with their start and end apart: 3 -> 0, of which waited for: 2 -> 0; matrix products, arithmetic and copies ran while one was open for 14% -> 0% of each run, Pallas kernels for 0% -> 0%
where the time goes in v2:
time: 62 us; the launch traced here: 61.7 us
  blocking collectives  44.6 us (72%)
  Pallas kernels  16.5 us (27%)
  between operations  0.63 us (1%)
    all_to_all x2, blocking collectives, exchange(): return lax.all_to_all(x, axis, split_axis=0, concat_axis=0, tiled=True)  44.6 us
    pallas_call x1, Pallas kernels, bin_sums(): pl.pallas_call(main_kernel, in_specs=[vmem, vmem], out_specs=vmem, out_sh...  10.5 us
    pallas_call x1, Pallas kernels, pack(): pl.pallas_call(pack_kernel, grid=(count // step,), in_specs=[pl.BlockSpec...  3.6 us
    pallas_call x1, Pallas kernels, finish(): pl.pallas_call(finish_kernel, in_specs=[vmem] * 5, out_specs=[vmem] * 2,...  2.45 us

profile of v2, /device:TPU:1, one launch (start us, length us, event | category | flops | bytes accessed | tf_op | source)
XLA Modules:
  0.0 61.7 jit_solution(12530355627723711730)
XLA Ops:
  0.6 3.6 %pack.1 = bf16[16,144,128]{2,1,0:T(8,128)(2,1)} custom-call(s32[1,128]{1,0:T(1,128)} %bitcast.13, s32[1,128]{1,0:T(1,128)} %bitcast.14, bf16[16,128,128]{2,1,0:T(8,128)(2,1)} %bitcast.10), custom_call_target="tpu_custom_call" | custom-call | tf_op jit(solution)/shard_map/pack/pallas_call | solution.py:42
  4.2 21.3 %all_to_all.16.y_ref = bf16[16,144,128]{2,1,0:T(8,128)(2,1)} all-to-all(bf16[16,144,128]{2,1,0:T(8,128)(2,1)} %pack.1), channel_id=1, replica_groups=mesh['loop'=16,'stack'=16] {'loop'}, dimensions={0} | all-to-all | bytes 1179648 | tf_op jit(solution)/shard_map/all_to_all | solution.py:258
  25.5 10.5 %bin_sums.1 = f32[256,8]{1,0:T(8,128)} custom-call(s32[1,128]{1,0:T(1,128)} %bitcast.15, bf16[16,144,128]{2,1,0:T(8,128)(2,1)} %all_to_all.16.y_ref), custom_call_target="tpu_custom_call" | custom-call | tf_op jit(solution)/shard_map/bin_sums/pallas_call | solution.py:192
  36.0 23.3 %all_to_all.17 = f32[256,1,8]{2,1,0:T(1,128)} all-to-all(f32[256,1,8]{2,1,0:T(1,128)} %bitcast.11), channel_id=1, replica_groups=mesh['loop'=16,'stack'=16] {'stack','loop'}, dimensions={0} | all-to-all | bytes 16384 | tf_op jit(solution)/shard_map/all_to_all | solution.py:258
  59.3 2.4 %finish.1 = (f32[8,128]{1,0:T(8,128)}, f32[8,128]{1,0:T(8,128)}) custom-call(f32[256,8]{1,0:T(8,128)} %bitcast.12, f32[16,128]{1,0:T(8,128)} %constant.8.clone.weight_ref, f32[64,16]{1,0:T(8,128)} %constant.9.clone.first_ref, f32[2,128,128]{2,1,0:T(8,128)} %constant.10.clone.twiddle_ref, f32[16,256]{1,0:T(8,128)} %constant.11.clone.last_ref), custom_call_target="tpu_custom_call" | custom-call | tf_op jit(solution)/shard_map/finish/pallas_call | solution.py:248

commit v3 on v2

--- a/solution.py
+++ b/solution.py
@@ -22,33 +22,42 @@
     return lax.dot_general(a, b, (((1,), (0,)), ((), ())), preferred_element_type=F32)
 
 
-def pack_kernel(loc_ref, valid_ref, x_ref, o_ref):
+PIECES = 4
+
+
+def pack_kernel(loc_ref, valid_ref, x_hbm, o_ref, x_ref, sems):
+    count = x_ref.shape[0]
+    size = count // PIECES
+    copies = [
+        pltpu.make_async_copy(x_hbm.at[pl.ds(i * size, size)], x_ref.at[pl.ds(i * size, size)], sems.at[i])
+        for i in range(PIECES)
+    ]
+    for copy in copies:
+        copy.start()
     row = iota((128, 128), 0)
     col = iota((128, 128), 1)
     valid = jnp.broadcast_to(valid_ref[...].astype(F32), (128, 128))
     pick = jnp.where(col == 16 * (row % 8) + row // 8, valid, 0.0).astype(BF16)
     jit = jnp.broadcast_to((loc_ref[...] & 1).astype(F32), (16, 128))
-    jit = jnp.where(iota((16, 128), 1) % 16 == iota((16, 128), 0), jit, 0.0).astype(BF16)
-    spread = jnp.where(col == row // 16, 1.0, 0.0).astype(BF16)
-    bits = dot_nn(jit, spread).astype(BF16)
-    for g in range(x_ref.shape[0]):
-        o_ref[g, 0:128] = dot_nt(pick, x_ref[g]).astype(BF16)
-        o_ref[g, 128:144] = bits
+    jit = jnp.where(iota((16, 128), 1) // 16 == iota((16, 128), 0), jit, 0.0).astype(BF16)
+    spread = jnp.where(col == row % 16, 1.0, 0.0).astype(BF16)
+    bits = dot_nn(jit, spread)[0:8].astype(BF16)
+    for i, copy in enumerate(copies):
+        copy.wait()
+        for g in range(i * size, (i + 1) * size):
+            o_ref[g, 0:128] = dot_nt(pick, x_ref[g]).astype(BF16)
+            o_ref[g, 128:136] = bits
 
 
 def pack(channel_loc, channel_valid, blocks):
     count = blocks.shape[0]
-    step = 4
+    vmem = pl.BlockSpec(memory_space=pltpu.VMEM)
     return pl.pallas_call(
         pack_kernel,
-        grid=(count // step,),
-        in_specs=[
-            pl.BlockSpec((1, 128), lambda i: (0, 0)),
-            pl.BlockSpec((1, 128), lambda i: (0, 0)),
-            pl.BlockSpec((step, 128, 128), lambda i: (i, 0, 0)),
-        ],
-        out_specs=pl.BlockSpec((step, 144, 128), lambda i: (i, 0, 0)),
-        out_shape=jax.ShapeDtypeStruct((count, 144, 128), BF16),
+        in_specs=[vmem, vmem, pl.BlockSpec(memory_space=pl.ANY)],
+        out_specs=vmem,
+        out_shape=pltpu.VMEM((count, 136, 128), BF16),
+        scratch_shapes=[pltpu.VMEM((count, 128, 128), BF16), pltpu.SemaphoreType.DMA((PIECES,))],
         name="pack",
     )(channel_loc.reshape(1, 128), channel_valid.reshape(1, 128), blocks)
 
@@ -76,92 +85,76 @@
     return dot_nn(hi, picks) + dot_nn(mid, picks) + dot_nn(rest, picks)
 
 
-CHUNK = 64
+CHUNK = 32
 NCHUNK = 128 // CHUNK
 
 
-def main_kernel(owner_row_ref, y_ref, o_ref, x_s, w_s, lin_s, acc_s, bits_s, pw_s):
+def main_kernel(owner_row_ref, y_ref, o_ref, x_s, w_s, lin_s, mask_s, lin_acc, acc_s, pw_s):
     lane = iota((128, 128), 1)
     row = iota((128, 128), 0)
     sign = jnp.where(row // 32 % 2 == 1, 1.0, -1.0)
     swap = jnp.where(row == jnp.where(lane // 32 % 2 == 0, lane + 32, lane - 32), sign, 0.0).astype(BF16)
-
-    bits = jnp.zeros((16, 128), F32)
-    for g in range(16):
-        piece = y_ref[g, 128:144, :].astype(F32)
-        bits = bits + (pltpu.roll(piece, 8 * g, 1) if g else piece)
-    bits_s[...] = bits
-    bits_t = jnp.transpose(jnp.concatenate([bits, jnp.zeros((112, 128), F32)], 0))
-
+    bits_t = y_ref[:, 128:136, :].astype(F32).reshape(128, 128)
+    bits = jnp.transpose(bits_t)
+    own = [jnp.where(lane // 64 == f, 1.0, 0.0).astype(BF16) for f in range(2)]
+
+    edge = jnp.where(row > lane, 1.0, jnp.where(row < lane, 0.0, -1.0))
     suffix = jnp.zeros((128, 128), F32)
     for r in reversed(range(16)):
+        late = jnp.broadcast_to(bits_t[:, r : r + 1], (128, 128))
+        gap = late - jnp.broadcast_to(bits[r : r + 1, :], (128, 128))
+        mask_s[r] = jnp.minimum(jnp.maximum(edge + gap, 0.0), 1.0)
         x = y_ref[:, 8 * r : 8 * r + 8, :].astype(F32).reshape(128, 128)
         xb = x.astype(BF16)
-        for c in range(NCHUNK):
-            x_s[c, CHUNK * r : CHUNK * r + CHUNK, :] = xb[CHUNK * c : CHUNK * c + CHUNK]
-        xs = dot_nn(xb, swap)
+        w_s[r, 0:128, :] = xb
+        w_s[r, 128:256, :] = dot_nn(xb, swap).astype(BF16)
+        hi = suffix.astype(BF16)
+        low = (suffix - hi.astype(F32)).astype(BF16)
         for f in range(2):
-            mine = lane // 64 == f
-            w_s[f, r, 0:128, :] = jnp.where(mine, x, 0.0).astype(BF16)
-            w_s[f, r, 128:256, :] = jnp.where(mine, xs, 0.0).astype(BF16)
-        hi = suffix.astype(BF16)
-        lin_s[r, :, 0:128] = hi
-        lin_s[r, :, 128:256] = (suffix - hi.astype(F32)).astype(BF16)
+            mine = xb * own[f]
+            for c in range(NCHUNK):
+                x_s[f, c, CHUNK * r : CHUNK * r + CHUNK, :] = mine[CHUNK * c : CHUNK * c + CHUNK]
+            lin_s[f, :, 256 * r : 256 * r + 128] = hi * own[f]
+            lin_s[f, :, 256 * r + 128 : 256 * r + 256] = low * own[f]
         suffix = suffix + x
 
-    keep_low = row > lane
+    acc_s[...] = jnp.zeros(acc_s.shape, F32)
+
     keep_diag = row >= lane
 
     def one_freq(f, carry):
         lin = jnp.zeros((128, 256), F32)
-        lin_same = jnp.zeros((128, 256), F32)
-        lin_jit = jnp.zeros((128, 256), F32)
-        acc_s[...] = jnp.zeros(acc_s.shape, F32)
+        lin_acc[...] = jnp.zeros(lin_acc.shape, F32)
         for r in range(16):
-            w = w_s[f, r]
-            lin = lin + dot_nt(lin_s[r], jnp.concatenate([w, w], 1))
-            jit_lane = jnp.broadcast_to(bits_s[r : r + 1, :], (CHUNK, 128))
+            w = w_s[r]
+            lin = lin + dot_nt(lin_s[f, :, 256 * r : 256 * r + 256], jnp.concatenate([w, w], 1))
             for c in range(NCHUNK):
                 rows = slice(CHUNK * c, CHUNK * c + CHUNK)
-                prod = dot_nt(x_s[c, CHUNK * r :, :], w)
-                acc_re = None
+                prod = dot_nt(x_s[f, c, CHUNK * r :, :], w)
+                mask = mask_s[r, rows]
                 for u in range(r, 16):
                     at = CHUNK * (u - r)
                     re = prod[at : at + CHUNK, 0:128]
                     im = prod[at : at + CHUNK, 128:256]
                     gain = lax.rsqrt(jnp.maximum(re * re + im * im, 1.0))
-                    pr = re * gain
-                    pi = im * gain
                     if u == r:
-                        mask = jit_lane * (1.0 - jnp.broadcast_to(bits_t[rows, r : r + 1], (CHUNK, 128)))
-                        acc_s[1, rows, 0:128] += pr
-                        acc_s[1, rows, 128:256] += pi
-                        acc_s[2, rows, 0:128] += pr * mask
-                        acc_s[2, rows, 128:256] += pi * mask
-                        acc_s[3, rows, 0:128] += re
-                        acc_s[3, rows, 128:256] += im
-                        acc_s[4, rows, 0:128] += re * mask
-                        acc_s[4, rows, 128:256] += im * mask
-                    elif acc_re is None:
-                        acc_re, acc_im = pr, pi
+                        lin_acc[rows, 0:128] += re * mask
+                        lin_acc[rows, 128:256] += im * mask
+                        gain = gain * mask
+                        acc_re = re * gain
+                        acc_im = im * gain
                     else:
-                        acc_re = acc_re + pr
-                        acc_im = acc_im + pi
-                if acc_re is not None:
-                    acc_s[0, rows, 0:128] += acc_re
-                    acc_s[0, rows, 128:256] += acc_im
+                        acc_re = acc_re + re * gain
+                        acc_im = acc_im + im * gain
+                acc_s[f, rows, 0:128] += acc_re
+                acc_s[f, rows, 128:256] += acc_im
         for part in range(4):
             cols = slice(128 * (part % 2), 128 * (part % 2) + 128)
-            conj = 1.0 if part % 2 == 0 else -1.0
-            if part < 2:
-                full, same, jit = lin[:, cols], acc_s[3, :, cols], acc_s[4, :, cols]
-            else:
-                full, same, jit = acc_s[0, :, cols], acc_s[1, :, cols], acc_s[2, :, cols]
-            low = jnp.where(keep_diag, full, 0.0) + jnp.where(keep_low, same - jit, 0.0)
-            up = jnp.where(keep_diag, 0.0, full * conj)
-            up = up + jnp.transpose(jnp.where(keep_low, jit, 0.0))
-            pw_s[f, part : part + 1, 0:128] = skew_sum(low)
-            pw_s[f, part : part + 1, 128:256] = skew_sum(up)
+            full = lin[:, cols] + lin_acc[:, cols] if part < 2 else acc_s[f, :, cols]
+            low = skew_sum(jnp.where(keep_diag, full, 0.0))
+            up = skew_sum(jnp.where(keep_diag, 0.0, full))
+            pw_s[f, part : part + 1, 0:128] = low
+            pw_s[f, part : part + 1, 128:256] = up if part % 2 == 0 else -up
         return carry
 
     pw_s[...] = jnp.zeros(pw_s.shape, F32)
@@ -193,13 +186,14 @@
         main_kernel,
         in_specs=[vmem, vmem],
         out_specs=vmem,
-        out_shape=jax.ShapeDtypeStruct((256, 8), F32),
+        out_shape=pltpu.VMEM((256, 8), F32),
         scratch_shapes=[
-            pltpu.VMEM((NCHUNK, 16 * CHUNK, 128), BF16),
-            pltpu.VMEM((2, 16, 256, 128), BF16),
-            pltpu.VMEM((16, 128, 256), BF16),
-            pltpu.VMEM((5, 128, 256), F32),
-            pltpu.VMEM((16, 128), F32),
+            pltpu.VMEM((2, NCHUNK, 16 * CHUNK, 128), BF16),
+            pltpu.VMEM((16, 256, 128), BF16),
+            pltpu.VMEM((2, 128, 16 * 256), BF16),
+            pltpu.VMEM((16, 128, 128), F32),
+            pltpu.VMEM((128, 256), F32),
+            pltpu.VMEM((2, 128, 256), F32),
             pltpu.VMEM((2, 8, 256), F32),
         ],
         name="bin_sums",
@@ -251,7 +245,11 @@
         out_specs=[vmem] * 2,
         out_shape=[jax.ShapeDtypeStruct((8, 128), F32)] * 2,
         name="finish",
-    )(mine, *[jnp.asarray(t) for t in lag_tables()])
+    )(mine, *[in_vmem(jnp.asarray(t)) for t in lag_tables()])
+
+
+def in_vmem(x):
+    return pltpu.with_memory_space_constraint(x, pltpu.VMEM)
 
 
 def exchange(x, axis):
@@ -261,8 +259,9 @@
 def on_device(spectra, channel_loc, channel_valid, bin_owner):
     blocks = spectra.reshape(lax.axis_size("loop"), 128, 128)
     received = exchange(pack(channel_loc, channel_valid, blocks), "loop")
+    received = in_vmem(received)
     sums = bin_sums(bin_owner, received)
-    linear, phase = finish(exchange(sums, ("stack", "loop")))
+    linear, phase = finish(in_vmem(exchange(sums, ("stack", "loop"))))
     return linear.reshape(1, 1, -1), phase.reshape(1, 1, -1)
 
 

time: 62 us -> 57.2 us (0.923)
  Pallas kernels: 16.5 us -> 12.8 us
  blocking collectives: 44.6 us -> 43.5 us
    pallas_call x1, Pallas kernels: 10.5 us -> 8.88 us  [bin_sums(): pl.pallas_call(main_kernel, in_specs=[vmem, vmem], out_specs=vmem, out_sh...]
    pallas_call x1, Pallas kernels: 3.6 us -> 2.45 us  [pack(): pl.pallas_call(pack_kernel, in_specs=[vmem, vmem, pl.BlockSpec(memory_spa...]
    all_to_all x2, blocking collectives: 44.6 us -> 43.5 us  [exchange(): return lax.all_to_all(x, axis, split_axis=0, concat_axis=0, tiled=True)]
    pallas_call x1, Pallas kernels: 2.45 us -> 1.46 us  [finish(): pl.pallas_call(finish_kernel, in_specs=[vmem] * 5, out_specs=[vmem] * 2,...]
where the time goes in v3:
time: 57.2 us; the launch traced here: 57 us
  blocking collectives  43.5 us (76%)
  Pallas kernels  12.8 us (22%)
  between operations  0.69 us (1%)
    all_to_all x2, blocking collectives, exchange(): return lax.all_to_all(x, axis, split_axis=0, concat_axis=0, tiled=True)  43.5 us
    pallas_call x1, Pallas kernels, bin_sums(): pl.pallas_call(main_kernel, in_specs=[vmem, vmem], out_specs=vmem, out_sh...  8.88 us
    pallas_call x1, Pallas kernels, pack(): pl.pallas_call(pack_kernel, in_specs=[vmem, vmem, pl.BlockSpec(memory_spa...  2.45 us
    pallas_call x1, Pallas kernels, finish(): pl.pallas_call(finish_kernel, in_specs=[vmem] * 5, out_specs=[vmem] * 2,...  1.46 us

profile of v3, /device:TPU:1, one launch (start us, length us, event | category | flops | bytes accessed | tf_op | source)
XLA Modules:
  0.0 57.0 jit_solution(7141418903585161335)
XLA Ops:
  0.6 2.4 %pack.1 = bf16[16,136,128]{2,1,0:T(8,128)(2,1)S(1)} custom-call(s32[1,128]{1,0:T(1,128)} %bitcast.13, s32[1,128]{1,0:T(1,128)} %bitcast.14, bf16[16,128,128]{2,1,0:T(8,128)(2,1)} %bitcast.12), custom_call_target="tpu_custom_call" | custom-call | tf_op jit(solution)/shard_map/pack/pallas_call | solution.py:55
  3.1 20.8 %all_to_all.16.y_ref = bf16[16,136,128]{2,1,0:T(8,128)(2,1)S(1)} all-to-all(bf16[16,136,128]{2,1,0:T(8,128)(2,1)S(1)} %pack.1), channel_id=1, replica_groups=mesh['loop'=16,'stack'=16] {'loop'}, dimensions={0} | all-to-all | bytes 1114112 | tf_op jit(solution)/shard_map/all_to_all | solution.py:256
  23.8 8.9 %bin_sums.1 = f32[256,8]{1,0:T(8,128)S(1)} custom-call(s32[1,128]{1,0:T(1,128)} %bitcast.15, bf16[16,136,128]{2,1,0:T(8,128)(2,1)S(1)} %all_to_all.16.y_ref), custom_call_target="tpu_custom_call" | custom-call | tf_op jit(solution)/shard_map/bin_sums/pallas_call | solution.py:185
  32.7 0.0 copy-start
  32.8 0.0 copy-start.1
  32.8 0.0 copy-start.2
  32.8 0.0 copy-start.3
  32.8 22.7 %all_to_all.17 = f32[256,1,8]{2,1,0:T(1,128)S(1)} all-to-all(f32[256,1,8]{2,1,0:T(1,128)S(1)} %bitcast.11), channel_id=1, replica_groups=mesh['loop'=16,'stack'=16] {'stack','loop'}, dimensions={0} | all-to-all | bytes 16384 | tf_op jit(solution)/shard_map/all_to_all | solution.py:256
  55.5 0.0 copy-done
  55.5 0.0 copy-done.1
  55.5 0.0 copy-done.2
  55.5 0.0 copy-done.3
  55.5 1.5 %finish.1 = (f32[8,128]{1,0:T(8,128)}, f32[8,128]{1,0:T(8,128)}) custom-call(f32[256,8]{1,0:T(8,128)S(1)} %bitcast.10, f32[16,128]{1,0:T(8,128)S(1)} %copy-done.3, f32[64,16]{1,0:T(8,128)S(1)} %copy-done.1, f32[2,128,128]{2,1,0:T(8,128)S(1)} %copy-done, f32[16,256]{1,0:T(8,128)S(1)} %copy-done.2), custom_call_target="tpu_custom_call" | custom-call | tf_op jit(solution)/shard_map/finish/pallas_call | solution.py:242
Async XLA Ops:
  32.7 22.8 %copy-start = (f32[2,128,128]{2,1,0:T(8,128)S(1)}, f32[2,128,128]{2,1,0:T(8,128)}, u32[]{:S(2)}) copy-start(f32[2,128,128]{2,1,0:T(8,128)} %constant.10.clone.twiddle_ref) | copy-start | bytes 393220
  32.8 22.8 %copy-start.1 = (f32[64,16]{1,0:T(8,128)S(1)}, f32[64,16]{1,0:T(8,128)}, u32[]{:S(2)}) copy-start(f32[64,16]{1,0:T(8,128)} %constant.9.clone.first_ref) | copy-start | bytes 12292
  32.8 22.8 %copy-start.2 = (f32[16,256]{1,0:T(8,128)S(1)}, f32[16,256]{1,0:T(8,128)}, u32[]{:S(2)}) copy-start(f32[16,256]{1,0:T(8,128)} %constant.11.clone.last_ref) | copy-start | bytes 49156
  32.8 22.8 %copy-start.3 = (f32[16,128]{1,0:T(8,128)S(1)}, f32[16,128]{1,0:T(8,128)}, u32[]{:S(2)}) copy-start(f32[16,128]{1,0:T(8,128)} %constant.8.clone.weight_ref) | copy-start | bytes 24580

commit v4 on v3

--- a/solution.py
+++ b/solution.py
@@ -25,15 +25,21 @@
 PIECES = 4
 
 
-def pack_kernel(loc_ref, valid_ref, x_hbm, o_ref, x_ref, sems):
+def pack_kernel(loc_hbm, valid_hbm, x_hbm, o_ref, loc_ref, valid_ref, x_ref, sems):
     count = x_ref.shape[0]
     size = count // PIECES
     copies = [
         pltpu.make_async_copy(x_hbm.at[pl.ds(i * size, size)], x_ref.at[pl.ds(i * size, size)], sems.at[i])
         for i in range(PIECES)
     ]
-    for copy in copies:
+    small = [
+        pltpu.make_async_copy(loc_hbm, loc_ref, sems.at[PIECES]),
+        pltpu.make_async_copy(valid_hbm, valid_ref, sems.at[PIECES + 1]),
+    ]
+    for copy in small + copies:
         copy.start()
+    for copy in small:
+        copy.wait()
     row = iota((128, 128), 0)
     col = iota((128, 128), 1)
     valid = jnp.broadcast_to(valid_ref[...].astype(F32), (128, 128))
@@ -51,13 +57,17 @@
 
 def pack(channel_loc, channel_valid, blocks):
     count = blocks.shape[0]
-    vmem = pl.BlockSpec(memory_space=pltpu.VMEM)
     return pl.pallas_call(
         pack_kernel,
-        in_specs=[vmem, vmem, pl.BlockSpec(memory_space=pl.ANY)],
-        out_specs=vmem,
+        in_specs=[pl.BlockSpec(memory_space=pl.ANY)] * 3,
+        out_specs=pl.BlockSpec(memory_space=pltpu.VMEM),
         out_shape=pltpu.VMEM((count, 136, 128), BF16),
-        scratch_shapes=[pltpu.VMEM((count, 128, 128), BF16), pltpu.SemaphoreType.DMA((PIECES,))],
+        scratch_shapes=[
+            pltpu.VMEM((1, 128), jnp.int32),
+            pltpu.VMEM((1, 128), jnp.int32),
+            pltpu.VMEM((count, 128, 128), BF16),
+            pltpu.SemaphoreType.DMA((PIECES + 2,)),
+        ],
         name="pack",
     )(channel_loc.reshape(1, 128), channel_valid.reshape(1, 128), blocks)
 
@@ -89,7 +99,9 @@
 NCHUNK = 128 // CHUNK
 
 
-def main_kernel(owner_row_ref, y_ref, o_ref, x_s, w_s, lin_s, mask_s, lin_acc, acc_s, pw_s):
+def main_kernel(owner_hbm, y_ref, o_ref, owner_row_ref, sem, x_s, w_s, lin_s, mask_s, lin_acc, acc_s, pw_s):
+    copy = pltpu.make_async_copy(owner_hbm, owner_row_ref, sem)
+    copy.start()
     lane = iota((128, 128), 1)
     row = iota((128, 128), 0)
     sign = jnp.where(row // 32 % 2 == 1, 1.0, -1.0)
@@ -122,9 +134,9 @@
 
     keep_diag = row >= lane
 
-    def one_freq(f, carry):
+    def one_freq(f):
         lin = jnp.zeros((128, 256), F32)
-        lin_acc[...] = jnp.zeros(lin_acc.shape, F32)
+        lin_acc[f] = jnp.zeros((128, 256), F32)
         for r in range(16):
             w = w_s[r]
             lin = lin + dot_nt(lin_s[f, :, 256 * r : 256 * r + 256], jnp.concatenate([w, w], 1))
@@ -138,8 +150,8 @@
                     im = prod[at : at + CHUNK, 128:256]
                     gain = lax.rsqrt(jnp.maximum(re * re + im * im, 1.0))
                     if u == r:
-                        lin_acc[rows, 0:128] += re * mask
-                        lin_acc[rows, 128:256] += im * mask
+                        lin_acc[f, rows, 0:128] += re * mask
+                        lin_acc[f, rows, 128:256] += im * mask
                         gain = gain * mask
                         acc_re = re * gain
                         acc_im = im * gain
@@ -150,15 +162,15 @@
                 acc_s[f, rows, 128:256] += acc_im
         for part in range(4):
             cols = slice(128 * (part % 2), 128 * (part % 2) + 128)
-            full = lin[:, cols] + lin_acc[:, cols] if part < 2 else acc_s[f, :, cols]
+            full = lin[:, cols] + lin_acc[f, :, cols] if part < 2 else acc_s[f, :, cols]
             low = skew_sum(jnp.where(keep_diag, full, 0.0))
             up = skew_sum(jnp.where(keep_diag, 0.0, full))
             pw_s[f, part : part + 1, 0:128] = low
             pw_s[f, part : part + 1, 128:256] = up if part % 2 == 0 else -up
-        return carry
 
     pw_s[...] = jnp.zeros(pw_s.shape, F32)
-    lax.fori_loop(0, 2, one_freq, 0)
+    for f in range(2):
+        one_freq(f)
 
     low_pick = jnp.where((lane + row) % 128 == 0, 1.0, 0.0)
     up_pick = jnp.where(row == lane + 1, 1.0, 0.0)
@@ -169,6 +181,7 @@
         part = [sums[8 * f + p : 8 * f + p + 1] for p in range(4)]
         power = part[2] * part[2] + part[3] * part[3]
         out += [part[0], part[1], part[0] * power, part[1] * power]
+    copy.wait()
     owner_row = jnp.broadcast_to(owner_row_ref[...], (128, 128))
     earlier = (owner_row == jnp.transpose(owner_row)) & (row < lane)
     rank = jnp.sum(jnp.where(earlier, 1.0, 0.0), 0, keepdims=True).astype(jnp.int32)
@@ -184,15 +197,17 @@
     vmem = pl.BlockSpec(memory_space=pltpu.VMEM)
     return pl.pallas_call(
         main_kernel,
-        in_specs=[vmem, vmem],
+        in_specs=[pl.BlockSpec(memory_space=pl.ANY), vmem],
         out_specs=vmem,
         out_shape=pltpu.VMEM((256, 8), F32),
         scratch_shapes=[
+            pltpu.VMEM((1, 128), jnp.int32),
+            pltpu.SemaphoreType.DMA(()),
             pltpu.VMEM((2, NCHUNK, 16 * CHUNK, 128), BF16),
             pltpu.VMEM((16, 256, 128), BF16),
             pltpu.VMEM((2, 128, 16 * 256), BF16),
             pltpu.VMEM((16, 128, 128), F32),
-            pltpu.VMEM((128, 256), F32),
+            pltpu.VMEM((2, 128, 256), F32),
             pltpu.VMEM((2, 128, 256), F32),
             pltpu.VMEM((2, 8, 256), F32),
         ],

time: 57.2 us -> 55.4 us (0.969)
  Pallas kernels: 12.8 us -> 11 us
    pallas_call x2, Pallas kernels: 11.3 us -> 9.56 us  [the longest x1 7.73 us: bin_sums(): pl.pallas_call(main_kernel, in_specs=[pl.BlockSpec(memory_space=pl.ANY),...]
where the time goes in v4:
time: 55.4 us; the launch traced here: 55.2 us
  blocking collectives  43.5 us (79%)
  Pallas kernels  11 us (20%)
  between operations  0.69 us (1%)
    all_to_all x2, blocking collectives, exchange(): return lax.all_to_all(x, axis, split_axis=0, concat_axis=0, tiled=True)  43.5 us
    pallas_call x1, Pallas kernels, bin_sums(): pl.pallas_call(main_kernel, in_specs=[pl.BlockSpec(memory_space=pl.ANY),...  7.73 us
    pallas_call x1, Pallas kernels, pack(): pl.pallas_call(pack_kernel, in_specs=[pl.BlockSpec(memory_space=pl.ANY)]...  1.83 us
    pallas_call x1, Pallas kernels, finish(): pl.pallas_call(finish_kernel, in_specs=[vmem] * 5, out_specs=[vmem] * 2,...  1.46 us

profile of v4, /device:TPU:1, one launch (start us, length us, event | category | flops | bytes accessed | tf_op | source)
XLA Modules:
  0.0 55.2 jit_solution(1175094792650549083)
XLA Ops:
  0.6 1.8 %pack.1 = bf16[16,136,128]{2,1,0:T(8,128)(2,1)S(1)} custom-call(s32[1,128]{1,0:T(1,128)} %bitcast.13, s32[1,128]{1,0:T(1,128)} %bitcast.14, bf16[16,128,128]{2,1,0:T(8,128)(2,1)} %bitcast.12), custom_call_target="tpu_custom_call" | custom-call | tf_op jit(solution)/shard_map/pack/pallas_call | solution.py:60
  2.5 20.8 %all_to_all.16.y_ref = bf16[16,136,128]{2,1,0:T(8,128)(2,1)S(1)} all-to-all(bf16[16,136,128]{2,1,0:T(8,128)(2,1)S(1)} %pack.1), channel_id=1, replica_groups=mesh['loop'=16,'stack'=16] {'loop'}, dimensions={0} | all-to-all | bytes 1114112 | tf_op jit(solution)/shard_map/all_to_all | solution.py:271
  23.2 7.7 %bin_sums.1 = f32[256,8]{1,0:T(8,128)S(1)} custom-call(s32[1,128]{1,0:T(1,128)} %bitcast.15, bf16[16,136,128]{2,1,0:T(8,128)(2,1)S(1)} %all_to_all.16.y_ref), custom_call_target="tpu_custom_call" | custom-call | tf_op jit(solution)/shard_map/bin_sums/pallas_call | solution.py:198
  31.0 0.0 copy-start
  31.0 0.0 copy-start.1
  31.0 0.0 copy-start.2
  31.0 0.0 copy-start.3
  31.0 22.7 %all_to_all.17 = f32[256,1,8]{2,1,0:T(1,128)S(1)} all-to-all(f32[256,1,8]{2,1,0:T(1,128)S(1)} %bitcast.11), channel_id=1, replica_groups=mesh['loop'=16,'stack'=16] {'stack','loop'}, dimensions={0} | all-to-all | bytes 16384 | tf_op jit(solution)/shard_map/all_to_all | solution.py:271
  53.8 0.0 copy-done
  53.8 0.0 copy-done.1
  53.8 0.0 copy-done.2
  53.8 0.0 copy-done.3
  53.8 1.5 %finish.1 = (f32[8,128]{1,0:T(8,128)}, f32[8,128]{1,0:T(8,128)}) custom-call(f32[256,8]{1,0:T(8,128)S(1)} %bitcast.10, f32[16,128]{1,0:T(8,128)S(1)} %copy-done.3, f32[64,16]{1,0:T(8,128)S(1)} %copy-done.1, f32[2,128,128]{2,1,0:T(8,128)S(1)} %copy-done, f32[16,256]{1,0:T(8,128)S(1)} %copy-done.2), custom_call_target="tpu_custom_call" | custom-call | tf_op jit(solution)/shard_map/finish/pallas_call | solution.py:257
Async XLA Ops:
  31.0 22.8 %copy-start = (f32[2,128,128]{2,1,0:T(8,128)S(1)}, f32[2,128,128]{2,1,0:T(8,128)}, u32[]{:S(2)}) copy-start(f32[2,128,128]{2,1,0:T(8,128)} %constant.10.clone.twiddle_ref) | copy-start | bytes 393220
  31.0 22.8 %copy-start.1 = (f32[64,16]{1,0:T(8,128)S(1)}, f32[64,16]{1,0:T(8,128)}, u32[]{:S(2)}) copy-start(f32[64,16]{1,0:T(8,128)} %constant.9.clone.first_ref) | copy-start | bytes 12292
  31.0 22.8 %copy-start.2 = (f32[16,256]{1,0:T(8,128)S(1)}, f32[16,256]{1,0:T(8,128)}, u32[]{:S(2)}) copy-start(f32[16,256]{1,0:T(8,128)} %constant.11.clone.last_ref) | copy-start | bytes 49156
  31.0 22.8 %copy-start.3 = (f32[16,128]{1,0:T(8,128)S(1)}, f32[16,128]{1,0:T(8,128)}, u32[]{:S(2)}) copy-start(f32[16,128]{1,0:T(8,128)} %constant.8.clone.weight_ref) | copy-start | bytes 24580

commit v5 on v4

--- a/solution.py
+++ b/solution.py
@@ -22,7 +22,7 @@
     return lax.dot_general(a, b, (((1,), (0,)), ((), ())), preferred_element_type=F32)
 
 
-PIECES = 4
+PIECES = 1
 
 
 def pack_kernel(loc_hbm, valid_hbm, x_hbm, o_ref, loc_ref, valid_ref, x_ref, sems):
@@ -232,21 +232,27 @@
     return [np.asarray(t, np.float32) for t in (weight, first, np.stack([t1, t2]), np.concatenate(last, 0))]
 
 
+def dot3(a, b, dim):
+    ah = a.astype(BF16)
+    al = (a - ah.astype(F32)).astype(BF16)
+    bh = b.astype(BF16)
+    bl = (b - bh.astype(F32)).astype(BF16)
+    dot = dot_nt if dim else dot_nn
+    return dot(ah, bh) + (dot(ah, bl) + dot(al, bh))
+
+
 def finish_kernel(x_ref, weight_ref, first_ref, twiddle_ref, last_ref, lin_ref, phase_ref):
     spread = jnp.where(iota((8, 128), 0) == iota((8, 128), 1) % 8, 1.0, 0.0).astype(BF16)
     wide = exact_dot(x_ref[...], spread)
     wide = jnp.where(iota((256, 128), 0) % 16 == iota((256, 128), 1) // 8, wide, 0.0)
     z = jnp.sum(wide.reshape(16, 16, 128), 1) * weight_ref[...]
-    high = lax.Precision.HIGHEST
-    v = jnp.dot(first_ref[...], z, precision=high, preferred_element_type=F32)
+    v = dot3(first_ref[...], z, 0)
     g = jnp.concatenate([v[0:32]] * 4, 0)
     h = jnp.concatenate([v[32:64]] * 4, 0)
     t1 = twiddle_ref[0]
     t2 = twiddle_ref[1]
     q = jnp.concatenate([g * t1 + h * t2, h * t1 - g * t2], 1)
-    series = lax.dot_general(
-        last_ref[...], q, (((1,), (1,)), ((), ())), precision=high, preferred_element_type=F32
-    )
+    series = dot3(last_ref[...], q, 1)
     for i, o_ref in enumerate((lin_ref, phase_ref)):
         c = series[8 * i : 8 * i + 8]
         o_ref[...] = c / jnp.sqrt(jnp.sum(c * c) * (1.0 / 1024) + 1e-06)

time: 55.4 us -> 55.1 us (level)
  no operation moved by 1% of the time
where the time goes in v5:
time: 55.1 us; the launch traced here: 54.9 us
  blocking collectives  43.5 us (79%)
  Pallas kernels  10.7 us (19%)
  between operations  0.69 us (1%)
    all_to_all x2, blocking collectives, exchange(): return lax.all_to_all(x, axis, split_axis=0, concat_axis=0, tiled=True)  43.5 us
    pallas_call x1, Pallas kernels, bin_sums(): pl.pallas_call(main_kernel, in_specs=[pl.BlockSpec(memory_space=pl.ANY),...  7.74 us
    pallas_call x1, Pallas kernels, pack(): pl.pallas_call(pack_kernel, in_specs=[pl.BlockSpec(memory_space=pl.ANY)]...  1.58 us
    pallas_call x1, Pallas kernels, finish(): pl.pallas_call(finish_kernel, in_specs=[vmem] * 5, out_specs=[vmem] * 2,...  1.37 us

profile of v5, /device:TPU:1, one launch (start us, length us, event | category | flops | bytes accessed | tf_op | source)
XLA Modules:
  0.0 54.9 jit_solution(1543235219136011220)
XLA Ops:
  0.6 1.6 %pack.1 = bf16[16,136,128]{2,1,0:T(8,128)(2,1)S(1)} custom-call(s32[1,128]{1,0:T(1,128)} %bitcast.13, s32[1,128]{1,0:T(1,128)} %bitcast.14, bf16[16,128,128]{2,1,0:T(8,128)(2,1)} %bitcast.12), custom_call_target="tpu_custom_call" | custom-call | tf_op jit(solution)/shard_map/pack/pallas_call | solution.py:60
  2.2 20.8 %all_to_all.16.y_ref = bf16[16,136,128]{2,1,0:T(8,128)(2,1)S(1)} all-to-all(bf16[16,136,128]{2,1,0:T(8,128)(2,1)S(1)} %pack.1), channel_id=1, replica_groups=mesh['loop'=16,'stack'=16] {'loop'}, dimensions={0} | all-to-all | bytes 1114112 | tf_op jit(solution)/shard_map/all_to_all | solution.py:277
  23.0 7.7 %bin_sums.1 = f32[256,8]{1,0:T(8,128)S(1)} custom-call(s32[1,128]{1,0:T(1,128)} %bitcast.15, bf16[16,136,128]{2,1,0:T(8,128)(2,1)S(1)} %all_to_all.16.y_ref), custom_call_target="tpu_custom_call" | custom-call | tf_op jit(solution)/shard_map/bin_sums/pallas_call | solution.py:198
  30.7 0.0 copy-start
  30.7 0.0 copy-start.1
  30.7 0.0 copy-start.2
  30.8 0.0 copy-start.3
  30.8 22.7 %all_to_all.17 = f32[256,1,8]{2,1,0:T(1,128)S(1)} all-to-all(f32[256,1,8]{2,1,0:T(1,128)S(1)} %bitcast.11), channel_id=1, replica_groups=mesh['loop'=16,'stack'=16] {'stack','loop'}, dimensions={0} | all-to-all | bytes 16384 | tf_op jit(solution)/shard_map/all_to_all | solution.py:277
  53.5 0.0 copy-done
  53.5 0.0 copy-done.1
  53.5 0.0 copy-done.2
  53.5 0.0 copy-done.3
  53.5 1.4 %finish.1 = (f32[8,128]{1,0:T(8,128)}, f32[8,128]{1,0:T(8,128)}) custom-call(f32[256,8]{1,0:T(8,128)S(1)} %bitcast.10, f32[16,128]{1,0:T(8,128)S(1)} %copy-done.3, f32[64,16]{1,0:T(8,128)S(1)} %copy-done.1, f32[2,128,128]{2,1,0:T(8,128)S(1)} %copy-done, f32[16,256]{1,0:T(8,128)S(1)} %copy-done.2), custom_call_target="tpu_custom_call" | custom-call | tf_op jit(solution)/shard_map/finish/pallas_call | solution.py:263
Async XLA Ops:
  30.7 22.8 %copy-start = (f32[2,128,128]{2,1,0:T(8,128)S(1)}, f32[2,128,128]{2,1,0:T(8,128)}, u32[]{:S(2)}) copy-start(f32[2,128,128]{2,1,0:T(8,128)} %constant.10.clone.twiddle_ref) | copy-start | bytes 393220
  30.7 22.8 %copy-start.1 = (f32[64,16]{1,0:T(8,128)S(1)}, f32[64,16]{1,0:T(8,128)}, u32[]{:S(2)}) copy-start(f32[64,16]{1,0:T(8,128)} %constant.9.clone.first_ref) | copy-start | bytes 12292
  30.7 22.8 %copy-start.2 = (f32[16,256]{1,0:T(8,128)S(1)}, f32[16,256]{1,0:T(8,128)}, u32[]{:S(2)}) copy-start(f32[16,256]{1,0:T(8,128)} %constant.11.clone.last_ref) | copy-start | bytes 49156
  30.8 22.8 %copy-start.3 = (f32[16,128]{1,0:T(8,128)S(1)}, f32[16,128]{1,0:T(8,128)}, u32[]{:S(2)}) copy-start(f32[16,128]{1,0:T(8,128)} %constant.8.clone.weight_ref) | copy-start | bytes 24580

commit v6 on v5

--- a/solution.py
+++ b/solution.py
@@ -126,8 +126,8 @@
             mine = xb * own[f]
             for c in range(NCHUNK):
                 x_s[f, c, CHUNK * r : CHUNK * r + CHUNK, :] = mine[CHUNK * c : CHUNK * c + CHUNK]
-            lin_s[f, :, 256 * r : 256 * r + 128] = hi * own[f]
-            lin_s[f, :, 256 * r + 128 : 256 * r + 256] = low * own[f]
+            lin_s[f, r, 0] = hi * own[f]
+            lin_s[f, r, 1] = low * own[f]
         suffix = suffix + x
 
     acc_s[...] = jnp.zeros(acc_s.shape, F32)
@@ -139,7 +139,7 @@
         lin_acc[f] = jnp.zeros((128, 256), F32)
         for r in range(16):
             w = w_s[r]
-            lin = lin + dot_nt(lin_s[f, :, 256 * r : 256 * r + 256], jnp.concatenate([w, w], 1))
+            lin = lin + dot_nt(jnp.concatenate([lin_s[f, r, 0], lin_s[f, r, 1]], 1), jnp.concatenate([w, w], 1))
             for c in range(NCHUNK):
                 rows = slice(CHUNK * c, CHUNK * c + CHUNK)
                 prod = dot_nt(x_s[f, c, CHUNK * r :, :], w)
@@ -205,7 +205,7 @@
             pltpu.SemaphoreType.DMA(()),
             pltpu.VMEM((2, NCHUNK, 16 * CHUNK, 128), BF16),
             pltpu.VMEM((16, 256, 128), BF16),
-            pltpu.VMEM((2, 128, 16 * 256), BF16),
+            pltpu.VMEM((2, 16, 2, 128, 128), BF16),
             pltpu.VMEM((16, 128, 128), F32),
             pltpu.VMEM((2, 128, 256), F32),
             pltpu.VMEM((2, 128, 256), F32),

time: 55.1 us -> 54.9 us (level)
  no operation moved by 1% of the time
where the time goes in v6:
time: 54.9 us; the launch traced here: 54.8 us
  blocking collectives  43.5 us (79%)
  Pallas kernels  10.5 us (19%)
  between operations  0.69 us (1%)
    all_to_all x2, blocking collectives, exchange(): return lax.all_to_all(x, axis, split_axis=0, concat_axis=0, tiled=True)  43.5 us
    pallas_call x1, Pallas kernels, bin_sums(): pl.pallas_call(main_kernel, in_specs=[pl.BlockSpec(memory_space=pl.ANY),...  7.59 us
    pallas_call x1, Pallas kernels, pack(): pl.pallas_call(pack_kernel, in_specs=[pl.BlockSpec(memory_space=pl.ANY)]...  1.58 us
    pallas_call x1, Pallas kernels, finish(): pl.pallas_call(finish_kernel, in_specs=[vmem] * 5, out_specs=[vmem] * 2,...  1.37 us

profile of v6, /device:TPU:1, one launch (start us, length us, event | category | flops | bytes accessed | tf_op | source)
XLA Modules:
  0.0 54.8 jit_solution(4254165727458320429)
XLA Ops:
  0.6 1.6 %pack.1 = bf16[16,136,128]{2,1,0:T(8,128)(2,1)S(1)} custom-call(s32[1,128]{1,0:T(1,128)} %bitcast.13, s32[1,128]{1,0:T(1,128)} %bitcast.14, bf16[16,128,128]{2,1,0:T(8,128)(2,1)} %bitcast.12), custom_call_target="tpu_custom_call" | custom-call | tf_op jit(solution)/shard_map/pack/pallas_call | solution.py:60
  2.2 20.8 %all_to_all.16.y_ref = bf16[16,136,128]{2,1,0:T(8,128)(2,1)S(1)} all-to-all(bf16[16,136,128]{2,1,0:T(8,128)(2,1)S(1)} %pack.1), channel_id=1, replica_groups=mesh['loop'=16,'stack'=16] {'loop'}, dimensions={0} | all-to-all | bytes 1114112 | tf_op jit(solution)/shard_map/all_to_all | solution.py:277
  23.0 7.6 %bin_sums.1 = f32[256,8]{1,0:T(8,128)S(1)} custom-call(s32[1,128]{1,0:T(1,128)} %bitcast.15, bf16[16,136,128]{2,1,0:T(8,128)(2,1)S(1)} %all_to_all.16.y_ref), custom_call_target="tpu_custom_call" | custom-call | tf_op jit(solution)/shard_map/bin_sums/pallas_call | solution.py:198
  30.6 0.0 copy-start
  30.6 0.0 copy-start.1
  30.6 0.0 copy-start.2
  30.6 0.0 copy-start.3
  30.6 22.7 %all_to_all.17 = f32[256,1,8]{2,1,0:T(1,128)S(1)} all-to-all(f32[256,1,8]{2,1,0:T(1,128)S(1)} %bitcast.11), channel_id=1, replica_groups=mesh['loop'=16,'stack'=16] {'stack','loop'}, dimensions={0} | all-to-all | bytes 16384 | tf_op jit(solution)/shard_map/all_to_all | solution.py:277
  53.4 0.0 copy-done
  53.4 0.0 copy-done.1
  53.4 0.0 copy-done.2
  53.4 0.0 copy-done.3
  53.4 1.4 %finish.1 = (f32[8,128]{1,0:T(8,128)}, f32[8,128]{1,0:T(8,128)}) custom-call(f32[256,8]{1,0:T(8,128)S(1)} %bitcast.10, f32[16,128]{1,0:T(8,128)S(1)} %copy-done.3, f32[64,16]{1,0:T(8,128)S(1)} %copy-done.1, f32[2,128,128]{2,1,0:T(8,128)S(1)} %copy-done, f32[16,256]{1,0:T(8,128)S(1)} %copy-done.2), custom_call_target="tpu_custom_call" | custom-call | tf_op jit(solution)/shard_map/finish/pallas_call | solution.py:263
Async XLA Ops:
  30.6 22.8 %copy-start = (f32[2,128,128]{2,1,0:T(8,128)S(1)}, f32[2,128,128]{2,1,0:T(8,128)}, u32[]{:S(2)}) copy-start(f32[2,128,128]{2,1,0:T(8,128)} %constant.10.clone.twiddle_ref) | copy-start | bytes 393220
  30.6 22.8 %copy-start.1 = (f32[64,16]{1,0:T(8,128)S(1)}, f32[64,16]{1,0:T(8,128)}, u32[]{:S(2)}) copy-start(f32[64,16]{1,0:T(8,128)} %constant.9.clone.first_ref) | copy-start | bytes 12292
  30.6 22.8 %copy-start.2 = (f32[16,256]{1,0:T(8,128)S(1)}, f32[16,256]{1,0:T(8,128)}, u32[]{:S(2)}) copy-start(f32[16,256]{1,0:T(8,128)} %constant.11.clone.last_ref) | copy-start | bytes 49156
  30.6 22.8 %copy-start.3 = (f32[16,128]{1,0:T(8,128)S(1)}, f32[16,128]{1,0:T(8,128)}, u32[]{:S(2)}) copy-start(f32[16,128]{1,0:T(8,128)} %constant.8.clone.weight_ref) | copy-start | bytes 24580

commit v7 on v6

--- a/solution.py
+++ b/solution.py
@@ -137,7 +137,7 @@
     def one_freq(f):
         lin = jnp.zeros((128, 256), F32)
         lin_acc[f] = jnp.zeros((128, 256), F32)
-        for r in range(16):
+        for r in reversed(range(16)):
             w = w_s[r]
             lin = lin + dot_nt(jnp.concatenate([lin_s[f, r, 0], lin_s[f, r, 1]], 1), jnp.concatenate([w, w], 1))
             for c in range(NCHUNK):

time: 54.9 us -> 55.1 us (level)
  no operation moved by 1% of the time
where the time goes in v7:
time: 55.1 us; the launch traced here: 54.9 us
  blocking collectives  43.5 us (79%)
  Pallas kernels  10.7 us (19%)
  between operations  0.69 us (1%)
    all_to_all x2, blocking collectives, exchange(): return lax.all_to_all(x, axis, split_axis=0, concat_axis=0, tiled=True)  43.5 us
    pallas_call x1, Pallas kernels, bin_sums(): pl.pallas_call(main_kernel, in_specs=[pl.BlockSpec(memory_space=pl.ANY),...  7.77 us
    pallas_call x1, Pallas kernels, pack(): pl.pallas_call(pack_kernel, in_specs=[pl.BlockSpec(memory_space=pl.ANY)]...  1.58 us
    pallas_call x1, Pallas kernels, finish(): pl.pallas_call(finish_kernel, in_specs=[vmem] * 5, out_specs=[vmem] * 2,...  1.37 us

profile of v7, /device:TPU:1, one launch (start us, length us, event | category | flops | bytes accessed | tf_op | source)
XLA Modules:
  0.0 54.9 jit_solution(1557009486608157479)
XLA Ops:
  0.6 1.6 %pack.1 = bf16[16,136,128]{2,1,0:T(8,128)(2,1)S(1)} custom-call(s32[1,128]{1,0:T(1,128)} %bitcast.13, s32[1,128]{1,0:T(1,128)} %bitcast.14, bf16[16,128,128]{2,1,0:T(8,128)(2,1)} %bitcast.12), custom_call_target="tpu_custom_call" | custom-call | tf_op jit(solution)/shard_map/pack/pallas_call | solution.py:60
  2.2 20.8 %all_to_all.16.y_ref = bf16[16,136,128]{2,1,0:T(8,128)(2,1)S(1)} all-to-all(bf16[16,136,128]{2,1,0:T(8,128)(2,1)S(1)} %pack.1), channel_id=1, replica_groups=mesh['loop'=16,'stack'=16] {'loop'}, dimensions={0} | all-to-all | bytes 1114112 | tf_op jit(solution)/shard_map/all_to_all | solution.py:277
  23.0 7.8 %bin_sums.1 = f32[256,8]{1,0:T(8,128)S(1)} custom-call(s32[1,128]{1,0:T(1,128)} %bitcast.15, bf16[16,136,128]{2,1,0:T(8,128)(2,1)S(1)} %all_to_all.16.y_ref), custom_call_target="tpu_custom_call" | custom-call | tf_op jit(solution)/shard_map/bin_sums/pallas_call | solution.py:198
  30.7 0.0 copy-start
  30.8 0.0 copy-start.1
  30.8 0.0 copy-start.2
  30.8 0.0 copy-start.3
  30.8 22.7 %all_to_all.17 = f32[256,1,8]{2,1,0:T(1,128)S(1)} all-to-all(f32[256,1,8]{2,1,0:T(1,128)S(1)} %bitcast.11), channel_id=1, replica_groups=mesh['loop'=16,'stack'=16] {'stack','loop'}, dimensions={0} | all-to-all | bytes 16384 | tf_op jit(solution)/shard_map/all_to_all | solution.py:277
  53.5 0.0 copy-done
  53.5 0.0 copy-done.1
  53.5 0.0 copy-done.2
  53.6 0.0 copy-done.3
  53.6 1.4 %finish.1 = (f32[8,128]{1,0:T(8,128)}, f32[8,128]{1,0:T(8,128)}) custom-call(f32[256,8]{1,0:T(8,128)S(1)} %bitcast.10, f32[16,128]{1,0:T(8,128)S(1)} %copy-done.3, f32[64,16]{1,0:T(8,128)S(1)} %copy-done.1, f32[2,128,128]{2,1,0:T(8,128)S(1)} %copy-done, f32[16,256]{1,0:T(8,128)S(1)} %copy-done.2), custom_call_target="tpu_custom_call" | custom-call | tf_op jit(solution)/shard_map/finish/pallas_call | solution.py:263
Async XLA Ops:
  30.7 22.8 %copy-start = (f32[2,128,128]{2,1,0:T(8,128)S(1)}, f32[2,128,128]{2,1,0:T(8,128)}, u32[]{:S(2)}) copy-start(f32[2,128,128]{2,1,0:T(8,128)} %constant.10.clone.twiddle_ref) | copy-start | bytes 393220
  30.8 22.8 %copy-start.1 = (f32[64,16]{1,0:T(8,128)S(1)}, f32[64,16]{1,0:T(8,128)}, u32[]{:S(2)}) copy-start(f32[64,16]{1,0:T(8,128)} %constant.9.clone.first_ref) | copy-start | bytes 12292
  30.8 22.8 %copy-start.2 = (f32[16,256]{1,0:T(8,128)S(1)}, f32[16,256]{1,0:T(8,128)}, u32[]{:S(2)}) copy-start(f32[16,256]{1,0:T(8,128)} %constant.11.clone.last_ref) | copy-start | bytes 49156
  30.8 22.8 %copy-start.3 = (f32[16,128]{1,0:T(8,128)S(1)}, f32[16,128]{1,0:T(8,128)}, u32[]{:S(2)}) copy-start(f32[16,128]{1,0:T(8,128)} %constant.8.clone.weight_ref) | copy-start | bytes 24580
